TPU v7x, 128 devices: a whole 4x4x4 slice. The times are simulated.
128 devices in a mesh: lat: 8 (over z_lo, x), lon: 16 (over z_hi, y, core).
Axes of the slice: x: 4, y: 4, z: 4 (z_hi: 2, z_lo: 2; z = z_hi * 2 + z_lo), core: 2. Of those that a mesh axis runs over, the one named last changes fastest.
Arguments:
- fields: bfloat16 [448, 896, 768], P('lat', 'lon'), may hold values from -6 to 6
- cotangent: bfloat16 [448, 896, 768], P('lat', 'lon'), may hold values from -6 to 6
- inner_weight: bfloat16 [8, 2, 96, 96], replicated, may hold values from -0.4375 to 0.4375
- outer_weight: bfloat16 [8, 2, 96, 96], replicated, may hold values from -0.4375 to 0.4375
Outputs:
- field_gradient: bfloat16 [448, 896, 768], P('lat', 'lon')
- inner_gradient: float32 [8, 2, 96, 96], replicated
- outer_gradient: float32 [8, 2, 96, 96], replicated
All inputs are finite; a program needn't handle non-finite values.
Results may differ from a plain program's by a relative error of at most 0.012.
Values may be sent and summed in bfloat16 or wider, within the bound.
A program may use at most 128 MiB of HBM per device.

v0:
```python
import math

import jax
import jax.numpy as jnp
from jax import lax
from jax.sharding import PartitionSpec as P

LATS = 448
LONS = 896
MODES = 128
BLOCKS = 8
BLOCK_W = 96


def trig_rows(row_ids, col_ids, period):
    phase = (row_ids[:, None] * col_ids[None, :] % period).astype(jnp.float32) * (
        2.0 * math.pi / period
    )
    factor = 1.0 / math.sqrt(period)
    return (
        (jnp.cos(phase) * factor).astype(jnp.bfloat16),
        (jnp.sin(phase) * factor).astype(jnp.bfloat16),
    )


def tables(row_total, col_total, period, col_first):
    row_ids = jnp.arange(row_total, dtype=jnp.int32)
    col_ids = col_first + jnp.arange(col_total, dtype=jnp.int32)
    return trig_rows(row_ids, col_ids, period)


def gelu_pair(value):
    cdf = 0.5 * (1.0 + jax.scipy.special.erf(value * 0.7071067811865476))
    density = jnp.exp(-0.5 * value * value) * 0.3989422804014327
    return (value * cdf, cdf + value * density)


def product(form, left, right):
    return jnp.einsum(form, left, right, preferred_element_type=jnp.float32)


def complex_apply(left_r, left_i, weight):
    real = product("pbi,bij->pbj", left_r, weight[:, 0]) - product(
        "pbi,bij->pbj", left_i, weight[:, 1]
    )
    imag = product("pbi,bij->pbj", left_r, weight[:, 1]) + product(
        "pbi,bij->pbj", left_i, weight[:, 0]
    )
    return (real, imag)


def complex_adjoint(adj_r, adj_i, weight):
    real = product("pbj,bij->pbi", adj_r, weight[:, 0]) + product(
        "pbj,bij->pbi", adj_i, weight[:, 1]
    )
    imag = product("pbj,bij->pbi", adj_i, weight[:, 0]) - product(
        "pbj,bij->pbi", adj_r, weight[:, 1]
    )
    return (real, imag)


def complex_outer(left_r, left_i, adj_r, adj_i):
    real = product("pbi,pbj->bij", left_r, adj_r) + product("pbi,pbj->bij", left_i, adj_i)
    imag = product("pbi,pbj->bij", left_r, adj_i) - product("pbi,pbj->bij", left_i, adj_r)
    return jnp.stack([real, imag], axis=1)


def local(fields, cotangent, inner_weight, outer_weight):
    lat_count = lax.axis_size("lat")
    lon_count = lax.axis_size("lon")
    row_count, col_count, width = fields.shape
    per_group = MODES // (lat_count * lon_count)
    slot_ids = jnp.arange(2 * MODES, dtype=jnp.int32)
    group_ids = slot_ids // (2 * per_group)
    part_ids = slot_ids // per_group % 2
    mode_ids = group_ids * per_group + slot_ids % per_group
    cos_rows, sin_rows = trig_rows(mode_ids, jnp.arange(LONS, dtype=jnp.int32), LONS)
    group_table = jnp.where((part_ids == 0)[:, None], cos_rows, -sin_rows)
    stacked = jnp.concatenate([fields, cotangent], axis=0).reshape(lon_count, -1, col_count, width)
    spectra = product(
        "kw,xhwc->xhkc",
        group_table,
        lax.all_to_all(stacked, "lon", split_axis=0, concat_axis=2, tiled=True),
    ).astype(jnp.bfloat16)
    spectra = spectra.reshape(spectra.shape[1], 2 * MODES, width)
    banded = lax.all_to_all(
        lax.all_to_all(spectra, "lon", split_axis=1, concat_axis=0, tiled=True),
        "lat",
        split_axis=1,
        concat_axis=0,
        tiled=True,
    )
    data = banded.reshape(lat_count, 2, row_count, -1)
    lat_cos, lat_sin = tables(LATS, LATS, LATS, 0)
    square = jnp.stack([lat_cos, lat_sin], axis=0)
    lat_table = square.reshape(2, LATS, lat_count, row_count)
    mixed = product("tmbr,bsrx->tmsx", lat_table, data).reshape(2, LATS, 2, 2, per_group, width)
    cos_part = mixed[0]
    sin_part = mixed[1]
    group_now = lax.axis_index("lon") * lat_count + lax.axis_index("lat")
    own_modes = group_now * per_group + jnp.arange(per_group, dtype=jnp.int32)
    weight_now = jnp.where(own_modes == 0, 1.0, 2.0).astype(jnp.bfloat16)[:, None]

    def blocked(value):
        return value.reshape(-1, BLOCKS, BLOCK_W)

    z_r = blocked((cos_part[:, 0, 0] + sin_part[:, 0, 1]).astype(jnp.bfloat16))
    z_i = blocked((cos_part[:, 0, 1] - sin_part[:, 0, 0]).astype(jnp.bfloat16))
    back_r = blocked((cos_part[:, 1, 0] + sin_part[:, 1, 1]).astype(jnp.bfloat16) * weight_now)
    back_i = blocked((cos_part[:, 1, 1] - sin_part[:, 1, 0]).astype(jnp.bfloat16) * weight_now)
    u_r, u_i = complex_apply(z_r, z_i, inner_weight)
    gelu_r, slope_r = gelu_pair(u_r)
    gelu_i, slope_i = gelu_pair(u_i)
    hidden_r = gelu_r.astype(jnp.bfloat16)
    hidden_i = gelu_i.astype(jnp.bfloat16)
    hidden_adj_r, hidden_adj_i = complex_adjoint(back_r, back_i, outer_weight)
    u_adj_r = (hidden_adj_r * slope_r).astype(jnp.bfloat16)
    u_adj_i = (hidden_adj_i * slope_i).astype(jnp.bfloat16)
    outer_part = complex_outer(hidden_r, hidden_i, back_r, back_i)
    inner_part = complex_outer(z_r, z_i, u_adj_r, u_adj_i)
    inner_total, outer_total = lax.psum((inner_part, outer_part), ("lat", "lon"))
    scale = 1.0 / math.sqrt(LATS * MODES)
    inner_gradient = inner_total * scale
    outer_gradient = outer_total * scale
    z_adj_r, z_adj_i = complex_adjoint(u_adj_r, u_adj_i, inner_weight)
    adj_stack = jnp.stack(
        [
            z_adj_r.astype(jnp.bfloat16).reshape(LATS, per_group, width),
            z_adj_i.astype(jnp.bfloat16).reshape(LATS, per_group, width),
        ],
        axis=1,
    )
    mixed_back = product("tmh,mx->thx", square, adj_stack.reshape(LATS, -1)).reshape(
        2, LATS, 2, per_group, width
    )
    adj_r = mixed_back[0][:, 0] - mixed_back[1][:, 1]
    adj_i = mixed_back[1][:, 0] + mixed_back[0][:, 1]
    spectral_adj = jnp.stack([adj_r, adj_i], axis=1).astype(jnp.bfloat16)
    returned = lax.all_to_all(spectral_adj, "lat", split_axis=0, concat_axis=2, tiled=True)
    col_first = lax.axis_index("lon") * col_count
    piece = lax.all_gather(returned, "lon", axis=2, tiled=True)
    amount = piece.shape[2]
    cos_piece, sin_piece = tables(amount, col_count, LONS, col_first)
    panel = jnp.concatenate([cos_piece, -sin_piece], axis=0)
    merged = piece.reshape(row_count, 2 * amount, width)
    summed = product("hkc,kw->hwc", merged, panel)
    field_gradient = summed.astype(jnp.bfloat16)
    return (field_gradient, inner_gradient, outer_gradient)


def solution(mesh):
    return jax.shard_map(
        local,
        mesh=mesh,
        in_specs=(P("lat", "lon", None), P("lat", "lon", None), P(), P()),
        out_specs=(P("lat", "lon", None), P(), P()),
        check_vma=False,
    )
```

profile of v0, /device:TPU:1, one launch (start us, length us, event | category | flops | bytes accessed | tf_op | source)
XLA Modules:
  0.0 657.7 jit_solution(12091927492638763055)
XLA Ops:
  8.0 9.0 %pad_maximum_fusion = bf16[112,56,768]{2,1,0:T(8,128)(2,1)} fusion(bf16[56,56,768]{2,1,0:T(8,128)(2,1)} %param.5, bf16[56,56,768]{2,1,0:T(8,128)(2,1)} %param.4), kind=kLoop, calls=%fused_computation | loop fusion | flops 4816896 | bytes 19267584 | tf_op jit(solution)/shard_map/concatenate | solution.py:79
  17.0 9.3 %all-to-all-start = ((bf16[16,7,56,768]{3,2,1,0:T(8,128)(2,1)}), bf16[16,7,56,768]{3,2,1,0:T(8,128)(2,1)}, u32[]{:S(2)}, u32[]{:S(2)}) async-start(bf16[16,7,56,768]{3,2,1,0:T(8,128)(2,1)} %bitcast.188), calls=%async_computation | async-start | bytes 19267584 | tf_op jit(solution)/shard_map/all_to_all | solution.py:83
  26.3 129.1 %all-to-all-done = bf16[16,7,56,768]{3,2,1,0:T(8,128)(2,1)} async-done(((bf16[16,7,56,768]{3,2,1,0:T(8,128)(2,1)}), bf16[16,7,56,768]{3,2,1,0:T(8,128)(2,1)}, u32[]{:S(2)}, u32[]{:S(2)}) %all-to-all-start) | async-done | bytes 9633824 | tf_op jit(solution)/shard_map/all_to_all | solution.py:83
  155.4 8.1 %copy.135 = bf16[1,7,16,56,768]{4,3,2,1,0:T(8,128)(2,1)} copy(bf16[1,7,16,56,768]{4,3,1,2,0:T(8,128)(2,1)} %bitcast.5) | data formatting | bytes 19267584 | tf_op jit(solution)/shard_map/all_to_all | solution.py:83
  163.5 13.6 %convert_bitcast_fusion.1 = bf16[7,256,768]{1,2,0:T(8,128)(2,1)} fusion(bf16[7,896,768]{2,1,0:T(8,128)(2,1)} %bitcast.212, s32[256]{0:T(256)S(1)} %and_select_fusion, pred[256]{0:T(512)(128)(4,1)S(1)} %fusion.104), kind=kOutput, calls=%fused_computation.6 | convolution fusion | flops 2471526400 | bytes 12387584 | tf_op jit(solution)/shard_map/kw,xhwc->xhkc/dot_general | solution.py:39
  181.0 45.3 %all_to_all.66 = bf16[7,256,768]{2,0,1:T(8,128)(2,1)S(1)} all-to-all(bf16[7,256,768]{2,0,1:T(8,128)(2,1)S(1)} %copy.137), channel_id=1, replica_groups=mesh['lat'=8,'lon'=16] {'lon'}, dimensions={1} | all-to-all | bytes 5505024 | tf_op jit(solution)/shard_map/all_to_all | solution.py:87
  229.3 4.7 all-to-all-start.2
  234.0 4.9 multiply_convert_fusion.4
  238.9 5.2 multiply_convert_fusion.3
  244.1 24.0 %all-to-all-done.2 = bf16[112,16,768]{2,0,1:T(8,128)(2,1)S(1)} async-done(((bf16[112,16,768]{2,0,1:T(8,128)(2,1)}), bf16[112,16,768]{2,0,1:T(8,128)(2,1)S(1)}, u32[]{:S(2)}, u32[]{:S(2)}) %all-to-all-start.2) | async-done | bytes 2752544 | tf_op jit(solution)/shard_map/all_to_all | solution.py:86
  271.8 7.3 %reshape.303 = bf16[8,2,56,1536]{3,2,1,0:T(8,128)(2,1)} reshape(bf16[8,112,2,768]{3,2,1,0:T(2,128)(2,1)} %bitcast.211) | data formatting | bytes 5505024 | tf_op jit(solution)/shard_map/reshape | solution.py:93
  279.0 4.8 convolution_bitcast_fusion
  283.9 5.2 fusion.112
  289.1 7.7 %squeeze.16 = f32[448,2,2,1,768]{4,2,0,1,3:T(2,128)} reshape(f32[1,448,2,1536]{3,1,2,0:T(8,128)} %get-tuple-element.23) | data formatting | bytes 11010048 | tf_op jit(solution)/shard_map/squeeze | solution.py:98
  296.8 8.6 %fusion.114 = (f32[448,1,1,1,768]{4,2,0,1,3:T(1,128)S(1)}, f32[448,1,1,1,768]{4,2,0,1,3:T(1,128)S(1)}, f32[448,1,1,1,768]{4,2,0,1,3:T(1,128)}, f32[448,1,1,1,768]{4,2,0,1,3:T(1,128)}) fusion(f32[448,2,2,1,768]{4,2,0,1,3:T(2,128)} %squeeze.16), kind=kLoop, calls=%fused_computation.168 | loop fusion | bytes 11010048 | tf_op jit(solution)/shard_map/slice | solution.py:109
  305.4 7.7 %squeeze.17 = f32[448,2,2,1,768]{4,2,0,1,3:T(2,128)} reshape(f32[1,448,2,1536]{3,1,2,0:T(8,128)} %get-tuple-element.24) | data formatting | bytes 11010048 | tf_op jit(solution)/shard_map/squeeze | solution.py:99
  313.1 9.1 %fusion.115 = (f32[448,1,1,1,768]{4,2,0,1,3:T(1,128)}, f32[448,1,1,1,768]{4,2,0,1,3:T(1,128)S(1)}, f32[448,1,1,1,768]{4,2,0,1,3:T(1,128)}, f32[448,1,1,1,768]{4,2,0,1,3:T(1,128)S(1)}) fusion(f32[448,2,2,1,768]{4,2,0,1,3:T(2,128)} %squeeze.17), kind=kLoop, calls=%fused_computation.169 | loop fusion | bytes 11010048 | tf_op jit(solution)/shard_map/slice | solution.py:109
  355.4 4.9 squeeze.23
  360.3 4.6 squeeze.22
  364.9 7.2 %fusion.23 = (bf16[448,1,1,768]{3,1,2,0:T(2,128)(2,1)S(1)}, bf16[448,1,1,768]{3,1,2,0:T(2,128)(2,1)S(1)}) fusion(f32[448,2,1,768]{3,1,2,0:T(2,128)} %bitcast.208, f32[448,2,1,768]{3,1,2,0:T(2,128)} %bitcast.209), kind=kLoop, calls=%fused_computation.41 | loop fusion | flops 1376256 | bytes 6881280 | tf_op jit(solution)/shard_map/convert
  376.4 5.2 all-to-all-start.3
  386.4 14.6 %all-to-all-done.3 = bf16[448,2,1,768]{3,1,2,0:T(2,128)(2,1)} async-done(((bf16[448,2,1,768]{3,1,2,0:T(2,128)(2,1)}), bf16[448,2,1,768]{3,1,2,0:T(2,128)(2,1)}, u32[]{:S(2)}, u32[]{:S(2)}) %all-to-all-start.3) | async-done | bytes 1376288 | tf_op jit(solution)/shard_map/all_to_all | solution.py:139
  404.6 229.0 %all-reduce.3.cloned.1.call-done = (f32[8,2,96,96]{3,2,0,1:T(8,128)}, f32[8,2,96,96]{3,2,0,1:T(8,128)}) async-done(((f32[8,2,96,96]{3,2,0,1:T(8,128)}, f32[8,2,96,96]{3,2,0,1:T(8,128)}), (f32[8,2,96,96]{3,2,0,1:T(8,128)}, f32[8,2,96,96]{3,2,0,1:T(8,128)})) %all-reduce.3.cloned.1.call-update) | async-done | bytes 1179664 | tf_op jit(solution)/shard_map/psum | solution.py:121
  636.8 13.3 %convert_bitcast_fusion = bf16[56,56,768]{2,1,0:T(8,128)(2,1)} fusion(bf16[56,256,768]{2,1,0:T(8,128)(2,1)} %bitcast.189, bf16[128,56]{0,1:T(8,128)(2,1)S(1)} %fusion.102, bf16[128,56]{0,1:T(8,128)(2,1)S(1)} %multiply_convert_fusion.7), kind=kOutput, calls=%fused_computation.2 | convolution fusion | flops 1235591168 | bytes 26865664 | tf_op jit(solution)/shard_map/hkc,kw->hwc/dot_general | solution.py:39
  (82 shorter events, 59.3 us)
Async XLA Ops:
  17.0 138.4 %all-to-all-start = ((bf16[16,7,56,768]{3,2,1,0:T(8,128)(2,1)}), bf16[16,7,56,768]{3,2,1,0:T(8,128)(2,1)}, u32[]{:S(2)}, u32[]{:S(2)}) async-start(bf16[16,7,56,768]{3,2,1,0:T(8,128)(2,1)} %bitcast.188), calls=%async_computation | async-start | bytes 19267584 | tf_op jit(solution)/shard_map/all_to_all | solution.py:83
  229.3 38.8 %all-to-all-start.2 = ((bf16[112,16,768]{2,0,1:T(8,128)(2,1)}), bf16[112,16,768]{2,0,1:T(8,128)(2,1)S(1)}, u32[]{:S(2)}, u32[]{:S(2)}) async-start(bf16[112,16,768]{2,0,1:T(8,128)(2,1)} %copy.140), calls=%async_computation.2 | async-start | bytes 5505024 | tf_op jit(solution)/shard_map/all_to_all | solution.py:86
  271.8 7.3 %copy-start.13 = (bf16[1,448,8,56]{1,3,2,0:T(8,128)(2,1)S(1)}, bf16[1,448,8,56]{1,3,2,0:T(8,128)(2,1)}, u32[]{:S(2)}) copy-start(bf16[1,448,8,56]{1,3,2,0:T(8,128)(2,1)} %get-tuple-element.38) | copy-start | bytes 1204228
  313.1 9.1 %copy-start.7 = (f32[448,1,1,1,768]{4,2,0,1,3:T(1,128)S(1)}, f32[448,1,1,1,768]{4,2,0,1,3:T(1,128)}, u32[]{:S(2)}) copy-start(f32[448,1,1,1,768]{4,2,0,1,3:T(1,128)} %get-tuple-element.32) | copy-start | bytes 4128772
  323.7 1.4 copy-start.4
  334.7 9.8 %copy-start = (bf16[448,1,1,1,768]{0,4,3,2,1:T(8,128)(2,1)}, bf16[448,1,1,1,768]{0,4,3,2,1:T(8,128)(2,1)S(1)}, u32[]{:S(2)}) copy-start(bf16[448,1,1,1,768]{0,4,3,2,1:T(8,128)(2,1)S(1)} %copy.145) | copy-start | bytes 2064388
  336.3 2.6 copy-start.2
  336.4 1.8 copy-start.6
  339.0 1.0 copy-start.14
  340.0 1.1 copy-start.3
  342.3 1.4 copy-start.5
  345.6 1.1 copy-start.1
  349.8 1.0 copy-start.8
  349.8 1.2 copy-start.9
  376.4 5.2 copy-start.10
  376.4 24.7 %all-to-all-start.3 = ((bf16[448,2,1,768]{3,1,2,0:T(2,128)(2,1)}), bf16[448,2,1,768]{3,1,2,0:T(2,128)(2,1)}, u32[]{:S(2)}, u32[]{:S(2)}) async-start(bf16[448,2,1,768]{3,1,2,0:T(2,128)(2,1)} %pad_maximum_fusion.2), calls=%async_computation.3 | async-start | bytes 2752512 | tf_op jit(solution)/shard_map/all_to_all | solution.py:139
  381.5 252.0 %all-reduce.3.cloned.1.call-start = ((), (), s32[]{:S(2)}) async-start(), calls=%async_computation.5 | async-start | bytes 3145728 | tf_op jit(solution)/shard_map/psum | solution.py:121
  383.9 1.0 copy-start.11
  385.9 250.9 %all-gather.3.cloned.1.call-start = ((), (), s32[]{:S(2)}) async-start(), calls=%async_computation.4 | async-start | bytes 23396352 | tf_op jit(solution)/shard_map/all_gather | solution.py:141
  633.5 2.2 copy-start.12
Sparse Core Ops, SparseCore 0:
  387.7 245.7 all-reduce.2
Sparse Core Ops, SparseCore 1:
  404.2 135.9 all-gather.2
where the time goes:
time: 666 us; the launch traced here: 658 us
  waiting for transfers between devices  397 us (60%)
  local copies, waits for them, and re-layouts  91.3 us (14%)
  matrix products  48.3 us (7%)
  blocking collectives  45.3 us (7%)
  other arithmetic  40.4 us (6%)
  starting transfers between devices  19.7 us (3%)
  between operations  15.9 us (2%)
    psum x1, waiting for transfers between devices, local(): lax.psum((inner_part, outer_part), ('lat', 'lon'))  229 us
    all_to_all x1, waiting for transfers between devices, local(): lax.all_to_all(stacked, 'lon', split_axis=0, concat_axis=2, tiled=True)  129 us
    dot_general x24, matrix products, product(): return jnp.einsum(form, left, right, preferred_element_type=jnp.float32)  48.3 us
    all_to_all x1, blocking collectives, local(): lax.all_to_all(spectra, 'lon', split_axis=1, concat_axis=0, tiled=True)  45.3 us
    all_to_all x1, waiting for transfers between devices, local(): lax.all_to_all(lax.all_to_all(spectra, 'lon', split_axis=1, concat_axis=0...  24 us
    all_to_all x1, waiting for transfers between devices, local(): lax.all_to_all(spectral_adj, 'lat', split_axis=0, concat_axis=2, tiled=True)  14.6 us
  transfers between devices with their start and end apart: 5, of which 4 were waited for; matrix products, arithmetic and copies ran while one was open for 3% of the time, Pallas kernels for 0%

commit v1 on v0

v1 whole, which is shorter than its diff:
```python
import functools
import math

import jax
import jax.numpy as jnp
import numpy as np
from jax import lax
from jax.experimental import pallas as pl
from jax.experimental.pallas import tpu as pltpu
from jax.sharding import PartitionSpec as P

LATS = 448
LONS = 896
MODES = 128
BLOCKS = 8
BLOCK_W = 96
MESH = pl.DeviceIdType.MESH
BF = jnp.bfloat16
F32 = jnp.float32


def trig(rows, cols, period):
    phase = (np.outer(rows, cols) % period) * (2.0 * np.pi / period)
    factor = 1.0 / math.sqrt(period)
    return np.cos(phase) * factor, np.sin(phase) * factor


def lon_rows(half):
    return half * 64 + np.arange(64)


def tables():
    forward = np.zeros((2, 2, 256, 448))
    inverse = np.zeros((2, 448, 256))
    for zh in range(2):
        cols = zh * 448 + np.arange(448)
        for place, half in enumerate((zh, 1 - zh)):
            ids = lon_rows(half)
            cos, sin = trig(ids, cols, LONS)
            both = np.stack([cos, -sin], axis=1).reshape(128, 448)
            weight = np.repeat(np.where(ids == 0, 1.0, 2.0), 2)[:, None]
            forward[0, zh, place * 128 : place * 128 + 128] = both
            forward[1, zh, place * 128 : place * 128 + 128] = both * weight
        for half in range(2):
            cos, sin = trig(lon_rows(half), cols, LONS)
            both = np.stack([cos, -sin], axis=1).reshape(128, 448)
            inverse[zh, :, half * 128 : half * 128 + 128] = both.T
    order = np.concatenate([np.arange(0, 448, 2), np.arange(1, 448, 2)])
    cos, sin = trig(np.arange(448), order, LATS)
    lat_forward = np.concatenate([cos, sin], axis=1)
    lat_inverse = np.concatenate([cos.T, sin.T], axis=1)
    place = np.zeros((2, 2, 256, 96))
    for parity in range(2):
        for j in range(192):
            channel = (j + 64 * parity) % 192
            place[parity, channel // 96, j, channel % 96] = 1.0
    cast = lambda a: jnp.asarray(a.astype(np.float32)).astype(BF)
    return tuple(cast(a) for a in (forward, lat_forward, lat_inverse, inverse, place))


def gelu_pair(value):
    cdf = 0.5 * (1.0 + lax.erf(value * 0.7071067811865476))
    density = jnp.exp(-0.5 * value * value) * 0.3989422804014327
    return value * cdf, cdf + value * density


def dot(a, b):
    return lax.dot_general(a, b, (((1,), (0,)), ((), ())), preferred_element_type=F32)


def dot_nt(a, b):
    return lax.dot_general(a, b, (((1,), (1,)), ((), ())), preferred_element_type=F32)


def dot_tn(a, b):
    return lax.dot_general(a, b, (((0,), (0,)), ((), ())), preferred_element_type=F32)


def low_half(shape):
    return lax.broadcasted_iota(jnp.int32, shape, len(shape) - 1) < 64


def swap_halves(first, second):
    low = low_half(first.shape)
    turned = pltpu.roll(jnp.where(low, second, first), 64, 1)
    return jnp.where(low, first, turned), jnp.where(low, turned, second)


def body(
    fields, cotangent, inner, outer, fwd, latf, latb, inv, place,
    out, grad,
    TS, PK, R, OWN, SND, ZR, SS, D, E, XB, ZB, HB, BB, UB, SL, AM, BM, W, SB, HR, GI, GO,
    tsem, raw_ss, rsem, z_ss, zsem, d_ss, dsem, w_ss, wsem, wz_ss, wzsem, o_ss, fsem, hsem, osem,
):
    lat = lax.axis_index("lat")
    lon = lax.axis_index("lon")
    zh = lon // 8
    s = lon % 8
    y = s // 2
    core = s % 2
    parity = y % 2
    d = 2 * lat + core
    my_tile = 3 * (y // 2) + 2 * parity
    zdev = (lat, (1 - zh) * 8 + s)

    def s_of(r):
        return (s + r) % 8

    def d_of(r):
        return (d + r) % 16

    def s_dev(s2):
        return (lat, zh * 8 + s2)

    def d_dev(d2):
        return (d2 // 2, zh * 8 + y * 2 + d2 % 2)

    def send(src, dst, send_sem, recv_sem, device):
        pltpu.make_async_remote_copy(
            src_ref=src, dst_ref=dst, send_sem=send_sem, recv_sem=recv_sem,
            device_id=device, device_id_type=MESH,
        ).start()

    def drain(ref, sem):
        pltpu.make_async_copy(ref, ref, sem).wait()

    sources = (fields, cotangent)
    for fc in range(2):
        for q in range(2):
            pltpu.make_async_copy(
                sources[fc].at[:, :, :, pl.ds(128 + 384 * q, 128)], TS.at[fc, :, :, q], tsem.at[fc]
            ).start()

    barrier = pltpu.get_barrier_semaphore()
    for r in range(1, 8):
        pl.semaphore_signal(barrier, inc=1, device_id=s_dev(s_of(r)), device_id_type=MESH)
    for r in range(1, 16):
        pl.semaphore_signal(barrier, inc=1, device_id=d_dev(d_of(r)), device_id_type=MESH)
    pl.semaphore_signal(barrier, inc=1, device_id=zdev, device_id_type=MESH)
    pl.semaphore_wait(barrier, 23)

    def issue(fc, jj):
        for kk in range(2):
            for i in range(2):
                g = 14 * kk + 2 * jj + i
                for q in range(2):
                    even, odd = swap_halves(
                        TS[fc, g, 0, q].astype(F32), TS[fc, g, 1, q].astype(F32)
                    )
                    PK[fc, g, 2 * q] = even.astype(BF)
                    PK[fc, g, 2 * q + 1] = odd.astype(BF)
        j = 7 * fc + jj
        for r in range(8):
            s2 = s_of(r)
            y2 = s2 // 2
            g0 = 14 * (s2 % 2) + 2 * jj
            lane = pl.multiple_of(128 * (3 * (y2 // 2) + 2 * (y2 % 2)), 128)
            pairs = (
                (sources[fc].at[pl.ds(g0, 2), :, :, pl.ds(lane, 128)], R.at[j, :, pl.ds(0, 2), s]),
                (PK.at[fc, pl.ds(g0, 2), y2], R.at[j, :, 2, s]),
            )
            for src, dst in pairs:
                if r == 0:
                    pltpu.make_async_copy(src, dst, rsem.at[j]).start()
                else:
                    send(src, dst, raw_ss, rsem.at[j], s_dev(s2))

    for fc in range(2):
        drain(TS.at[fc], tsem.at[fc])

        @pl.loop(0, 7)
        def _(jj, fc=fc):
            issue(fc, jj)

    for refs, target in ((inner, AM), (outer, BM)):
        for part in range(2):
            total = None
            for b in range(2):
                spot = place[parity, b]
                moved = dot_nt(dot(spot, refs[2 * y + b, part]).astype(BF), spot)
                total = moved if total is None else total + moved
            total = total.astype(BF)
            if part == 0:
                target[0:256, 0:256] = total
                target[256:512, 256:512] = total
            else:
                target[0:256, 256:512] = total
                target[256:512, 0:256] = -total

    def stage_b(t):
        fc = t // 7
        drain(R.at[t], rsem.at[t])
        table = fwd[fc, zh]
        for i in range(2):
            data = jnp.concatenate([R[t, i, u].reshape(448, 128) for u in range(3)], axis=1)
            part = dot(table, data)
            OWN[t % 2, i] = part[0:128]
            SND[t, i] = part[128:256].astype(BF)
        send(SND.at[t], ZR.at[t], z_ss, zsem.at[t], zdev)

    def stage_c(t):
        fc = t // 7
        jj = t % 7
        drain(ZR.at[t], zsem.at[t])
        for i in range(2):
            total = OWN[t % 2, i] + ZR[t, i].astype(F32)
            SS[t, i] = total.astype(BF).reshape(16, 8, 384)
        for r in range(16):
            d2 = d_of(r)
            src = SS.at[t, :, d2]
            dst = D.at[fc, d, pl.ds(2 * jj, 2)]
            if r == 0:
                pltpu.make_async_copy(src, dst, dsem.at[fc]).start()
            else:
                send(src, dst, d_ss, dsem.at[fc], d_dev(d2))

    def unpack(fc):
        drain(D.at[fc], dsem.at[fc])

        @pl.loop(0, 16)
        def _(dd):
            block = D[fc, dd].reshape(112, 384)
            for u in range(3):
                E[u, pl.ds(pl.multiple_of(112 * dd, 8), 112), :] = block[:, 128 * u : 128 * u + 128].astype(F32)

    def spread(m):
        for part in range(2):
            a, b, c = (E[u, pl.ds(2 * m + part, 224, stride=8), :] for u in range(3))
            turned = pltpu.roll(c, 64, 1)
            whole = jnp.concatenate(
                [jnp.concatenate([a, c], axis=1), jnp.concatenate([b, turned], axis=1)], axis=0
            )
            if part == 0:
                XB[0:448, 0:256] = whole.astype(BF)
                XB[448:896, 256:512] = (-whole).astype(BF)
            else:
                XB[0:448, 256:512] = whole.astype(BF)
                XB[448:896, 0:256] = whole.astype(BF)

    def fields_side():
        unpack(0)

        @pl.loop(0, 4)
        def _(m):
            spread(m)
            z = dot(latf[...], XB[...]).astype(BF)
            ZB[m] = z
            gelu, slope = gelu_pair(dot(z, AM[...]))
            HB[m] = gelu.astype(BF)
            SL[m] = slope

    @pl.loop(0, 10)
    def _(t):
        stage_b(t)

        @pl.when(t > 0)
        def _():
            stage_c(t - 1)

    fields_side()

    @pl.loop(10, 14)
    def _(t):
        stage_b(t)
        stage_c(t - 1)

    stage_c(13)
    unpack(1)

    @pl.loop(0, 4)
    def _(m):
        spread(m)
        back = dot(latf[...], XB[...]).astype(BF)
        BB[m] = back
        u_adj = (dot_nt(back, BM[...]) * SL[m]).astype(BF)
        UB[m] = u_adj
        z_adj = dot_nt(u_adj, AM[...])
        XB[0:448, :] = z_adj.astype(BF)
        XB[448:896, 0:256] = (-z_adj[:, 256:512]).astype(BF)
        XB[448:896, 256:512] = z_adj[:, 0:256].astype(BF)
        adj = dot(latb[...], XB[...])
        for part in range(2):
            own = adj[:, 256 * part : 256 * part + 256]
            c0 = own[0:224, 128:256]
            c1 = pltpu.roll(own[224:448, 128:256], 64, 1)
            rows = pl.ds(2 * m + part, 224, stride=8)
            E[0, rows, :] = own[0:224, 0:128]
            E[1, rows, :] = own[224:448, 0:128]
            E[2, rows, :] = jnp.where(low_half(c0.shape), c0, c1)

    @pl.loop(0, 16)
    def _(dd):
        for u in range(3):
            block = E[u, pl.ds(pl.multiple_of(112 * dd, 8), 112), :]
            SB[dd, :, :, 128 * u : 128 * u + 128] = block.reshape(14, 8, 128).astype(BF)

    for half in range(2):
        for r in range(16):
            d2 = d_of(r)
            src = SB.at[d2, pl.ds(7 * half, 7)]
            dst = W.at[pl.ds(7 * half, 7), zh * 16 + d]
            if r == 0:
                pltpu.make_async_copy(src, dst, wsem.at[half]).start()
            else:
                send(src, dst, w_ss, wsem.at[half], d_dev(d2))

    GI[...] = jnp.zeros_like(GI)
    GO[...] = jnp.zeros_like(GO)

    @pl.loop(0, 4)
    def _(m):
        GI[...] += dot_tn(ZB[m], UB[m])
        GO[...] += dot_tn(HB[m], BB[m])

    for kind, ref in enumerate((GI, GO)):
        for part in range(2):
            if part == 0:
                total = ref[0:256, 0:256] + ref[256:512, 256:512]
            else:
                total = ref[0:256, 256:512] - ref[256:512, 0:256]
            for b in range(2):
                spot = place[parity, b].astype(F32)
                rows = lax.dot_general(
                    spot, total, (((0,), (0,)), ((), ())),
                    precision=lax.Precision.HIGHEST, preferred_element_type=F32,
                )
                grad[2 * kind + part, b] = lax.dot_general(
                    rows, spot, (((1,), (0,)), ((), ())),
                    precision=lax.Precision.HIGHEST, preferred_element_type=F32,
                )

    for half in range(2):
        mine = W.at[pl.ds(7 * half, 7), pl.ds(16 * zh, 16)]
        drain(mine, wsem.at[half])
        send(mine, mine, wz_ss, wzsem.at[half], zdev)

    for half in range(2):
        drain(W.at[pl.ds(7 * half, 7), pl.ds(0, 16)], wzsem.at[half])

        @pl.loop(7 * half, 7 * half + 7)
        def _(g):
            piece = dot(inv[zh], W[g].reshape(256, 384)).astype(BF)
            for u in range(3):
                R[g, 0, u] = piece[:, 128 * u : 128 * u + 128].reshape(8, 56, 128)
            for r in range(8):
                s2 = s_of(r)
                lane = pl.multiple_of(128 * my_tile, 128)
                full = (R.at[g, 0, pl.ds(0, 2), s2], out.at[14 * core + g, :, :, pl.ds(lane, 128)])
                part = (R.at[g, 0, 2, s2], HR.at[y, core, g])
                if r == 0:
                    pltpu.make_async_copy(*full, fsem).start()
                    pltpu.make_async_copy(*part, hsem.at[g]).start()
                else:
                    send(*full, o_ss, fsem, s_dev(s2))
                    send(*part, o_ss, hsem.at[g], s_dev(s2))

    @pl.loop(0, 14)
    def _(g):
        drain(HR.at[:, :, g], hsem.at[g])
        for kk in range(2):
            for q in range(2):
                first, second = swap_halves(
                    HR[2 * q, kk, g].astype(F32), HR[2 * q + 1, kk, g].astype(F32)
                )
                TS[0, 14 * kk + g, 0, q] = first.astype(BF)
                TS[0, 14 * kk + g, 1, q] = second.astype(BF)

    for q in range(2):
        pltpu.make_async_copy(
            TS.at[0, :, :, q], out.at[:, :, :, pl.ds(128 + 384 * q, 128)], osem
        ).start()
    drain(TS.at[0], osem)
    drain(out.at[:, :, :, pl.ds(0, 512)], fsem)
    drain(R.at[:, :, :, pl.ds(0, 7)], raw_ss)
    drain(SND, z_ss)
    drain(SS.at[:, :, pl.ds(0, 15)], d_ss)
    drain(SB.at[pl.ds(0, 15)], w_ss)
    drain(W.at[:, pl.ds(0, 16)], wz_ss)
    drain(R.at[:, 0, :, pl.ds(0, 7)], o_ss)


def step(fields, cotangent, inner, outer):
    dma = pltpu.SemaphoreType.DMA
    anyspace = pl.BlockSpec(memory_space=pl.ANY)
    vmem = pl.BlockSpec(memory_space=pltpu.VMEM)
    scratch = [
        pltpu.VMEM((2, 28, 2, 2, 56, 128), BF),
        pltpu.VMEM((2, 28, 4, 56, 128), BF),
        pltpu.VMEM((14, 2, 3, 8, 56, 128), BF),
        pltpu.VMEM((2, 2, 128, 384), F32),
        pltpu.VMEM((14, 2, 128, 384), BF),
        pltpu.VMEM((14, 2, 128, 384), BF),
        pltpu.VMEM((14, 2, 16, 8, 384), BF),
        pltpu.VMEM((2, 16, 14, 8, 384), BF),
        pltpu.VMEM((3, 1792, 128), F32),
        pltpu.VMEM((896, 512), BF),
        pltpu.VMEM((4, 448, 512), BF),
        pltpu.VMEM((4, 448, 512), BF),
        pltpu.VMEM((4, 448, 512), BF),
        pltpu.VMEM((4, 448, 512), BF),
        pltpu.VMEM((4, 448, 512), F32),
        pltpu.VMEM((512, 512), BF),
        pltpu.VMEM((512, 512), BF),
        pltpu.VMEM((14, 32, 8, 384), BF),
        pltpu.VMEM((16, 14, 8, 384), BF),
        pltpu.VMEM((4, 2, 14, 56, 128), BF),
        pltpu.VMEM((512, 512), F32),
        pltpu.VMEM((512, 512), F32),
        dma((2,)), dma, dma((14,)), dma, dma((14,)), dma, dma((2,)), dma, dma((2,)),
        dma, dma((2,)), dma, dma, dma((14,)), dma,
    ]
    return pl.pallas_call(
        body,
        out_shape=(
            jax.ShapeDtypeStruct((28, 2, 56, 768), BF),
            jax.ShapeDtypeStruct((4, 2, 96, 96), F32),
        ),
        in_specs=[anyspace] * 2 + [vmem] * 7,
        out_specs=(anyspace, vmem),
        scratch_shapes=scratch,
        compiler_params=pltpu.CompilerParams(
            collective_id=0, has_side_effects=True, vmem_limit_bytes=67043328
        ),
        name="spectral_step",
    )(fields, cotangent, inner, outer, *tables())


def local(fields, cotangent, inner_weight, outer_weight):
    field_gradient, part = step(
        fields.reshape(28, 2, 56, 768),
        cotangent.reshape(28, 2, 56, 768),
        inner_weight,
        outer_weight,
    )
    y = lax.axis_index("lon") % 8 // 2
    part = part * (1.0 / math.sqrt(LATS * MODES))
    part = part.reshape(2, 2, 2, BLOCK_W, BLOCK_W).transpose(0, 2, 1, 3, 4)
    mine = jnp.where(jnp.arange(4)[None, :, None, None, None, None] == y, part[:, None], 0.0)
    total = lax.psum(mine.reshape(2, BLOCKS, 2, BLOCK_W, BLOCK_W), ("lat", "lon"))
    return field_gradient.reshape(fields.shape), total[0], total[1]


def solution(mesh):
    return jax.shard_map(
        local,
        mesh=mesh,
        in_specs=(P("lat", "lon", None), P("lat", "lon", None), P(), P()),
        out_specs=(P("lat", "lon", None), P(), P()),
        check_vma=False,
    )
```

time: 666 us -> 401 us (0.60); the launches traced: 658 us -> 400 us
  waiting for transfers between devices: 397 us -> 149 us
  Pallas kernels: 0 us -> 226 us
  local copies, waits for them, and re-layouts: 91.3 us -> 7.91 us
  matrix products: 48.3 us -> 0 us
  blocking collectives: 45.3 us -> 0 us
  other arithmetic: 40.4 us -> 2.46 us
  starting transfers between devices: 19.7 us -> 0.04 us
    pallas_call x0 -> x1, Pallas kernels: none -> 226 us  [step(): pl.pallas_call(body, out_shape=(jax.ShapeDtypeStruct((28, 2, 56, 768), BF...]
    all_to_all x3 -> x0, waiting for transfers between devices: 168 us -> none  [the longest x1 129 us: local(): lax.all_to_all(stacked, 'lon', split_axis=0, concat_axis=2, tiled=True)]
    psum x1, waiting for transfers between devices: 229 us -> 149 us  [local(): lax.psum(mine.reshape(2, BLOCKS, 2, BLOCK_W, BLOCK_W), ('lat', 'lon'))]
    dot_general x24 -> x0, matrix products: 48.3 us -> none  [product(): return jnp.einsum(form, left, right, preferred_element_type=jnp.float32)]
    all_to_all x1 -> x0, blocking collectives: 45.3 us -> none  [local(): lax.all_to_all(spectra, 'lon', split_axis=1, concat_axis=0, tiled=True)]
    slice x4 -> x0, local copies, waits for them, and re-layouts: 25.8 us -> none  [the longest x1 9.13 us: local(): sin_part[:, 1, 1]]
    squeeze x4 -> x1, local copies, waits for them, and re-layouts: 24.9 us -> 2.65 us  [local(): return (field_gradient.reshape(fields.shape), total[0], total[1])]
    all_to_all x3 -> x0, starting transfers between devices: 19.1 us -> none  [the longest x1 9.29 us: local(): lax.all_to_all(stacked, 'lon', split_axis=0, concat_axis=2, tiled=True)]
  transfers between devices with their start and end apart: 5 -> 1, of which waited for: 4 -> 1; matrix products, arithmetic and copies ran while one was open for 3% -> 0% of each run, Pallas kernels for 0% -> 0%
where the time goes in v1:
time: 401 us; the launch traced here: 400 us
  Pallas kernels  226 us (56%)
  waiting for transfers between devices  149 us (37%)
  between operations  14.1 us (4%)
  local copies, waits for them, and re-layouts  7.91 us (2%)
    pallas_call x1, Pallas kernels, step(): pl.pallas_call(body, out_shape=(jax.ShapeDtypeStruct((28, 2, 56, 768), BF...  226 us
    psum x1, waiting for transfers between devices, local(): lax.psum(mine.reshape(2, BLOCKS, 2, BLOCK_W, BLOCK_W), ('lat', 'lon'))  149 us
  transfers between devices with their start and end apart: 1, of which 1 were waited for; matrix products, arithmetic and copies ran while one was open for 0% of the time, Pallas kernels for 0%

profile of v1, /device:TPU:1, one launch (start us, length us, event | category | flops | bytes accessed | tf_op | source)
XLA Modules:
  0.0 400.3 jit_solution(6304658353575866379)
XLA Ops:
  7.2 0.0 all-reduce.2.cloned.1.call-start
  7.2 226.4 %spectral_step.1 = (bf16[28,2,56,768]{3,2,1,0:T(8,128)(2,1)}, f32[4,2,96,96]{3,2,1,0:T(8,128)}) custom-call(bf16[28,2,56,768]{3,2,1,0:T(8,128)(2,1)} %bitcast.13, bf16[28,2,56,768]{3,2,1,0:T(8,128)(2,1)} %bitcast.14, bf16[8,2,96,96]{3,2,1,0:T(8,128)(2,1)} %inner.1, bf16[8,2,96,96]{3,2,1,0:T(8,128)(2,1)} %outer.1, bf16[2,2,256,448]{3,2,1,0:T(8,128)(2,1)} %constant.51.fwd, ...), custom_call_target="tpu_custom_call" | custom-call | tf_op jit(solution)/shard_map/spectral_step/pallas_call | solution.py:412
  233.6 1.0 broadcast_multiply_fusion
  234.7 0.1 broadcast_in_dim.28
  234.8 0.1 broadcast_in_dim.29
  234.9 0.2 broadcast_in_dim.31
  235.1 1.4 broadcast_select_fusion
  236.5 0.0 all-reduce.2.cloned.1.call-update
  236.5 149.4 %all-reduce.2.cloned.1.call-done = f32[2,8,2,96,96]{4,3,2,1,0:T(8,128)} async-done(((f32[2,8,2,96,96]{4,3,2,1,0:T(8,128)}), f32[2,8,2,96,96]{4,3,2,1,0:T(8,128)}) %all-reduce.2.cloned.1.call-update) | async-done | bytes 1179664 | tf_op jit(solution)/shard_map/psum | solution.py:439
  385.9 2.7 slice_bitcast_fusion
  388.6 4.9 %copy.15 = bf16[56,56,768]{2,1,0:T(8,128)(2,1)} copy(bf16[56,56,768]{2,1,0:T(8,128)(2,1)} %bitcast.12) | data formatting | bytes 9633792
  (2 shorter events, 0.0 us)
Async XLA Ops:
  7.2 378.8 %all-reduce.2.cloned.1.call-start = ((), (), s32[]{:S(2)}) async-start(), calls=%async_computation | async-start | bytes 3145728 | tf_op jit(solution)/shard_map/psum | solution.py:439
Sparse Core Ops, SparseCore 0:
  236.6 149.2 all-reduce.1

commit v2 on v1

--- a/solution.py
+++ b/solution.py
@@ -1,4 +1,3 @@
-import functools
 import math
 
 import jax
@@ -30,32 +29,18 @@
 
 
 def tables():
-    forward = np.zeros((2, 2, 256, 448))
-    inverse = np.zeros((2, 448, 256))
+    forward = np.zeros((2, 256, 448))
     for zh in range(2):
         cols = zh * 448 + np.arange(448)
         for place, half in enumerate((zh, 1 - zh)):
-            ids = lon_rows(half)
-            cos, sin = trig(ids, cols, LONS)
-            both = np.stack([cos, -sin], axis=1).reshape(128, 448)
-            weight = np.repeat(np.where(ids == 0, 1.0, 2.0), 2)[:, None]
-            forward[0, zh, place * 128 : place * 128 + 128] = both
-            forward[1, zh, place * 128 : place * 128 + 128] = both * weight
-        for half in range(2):
             cos, sin = trig(lon_rows(half), cols, LONS)
             both = np.stack([cos, -sin], axis=1).reshape(128, 448)
-            inverse[zh, :, half * 128 : half * 128 + 128] = both.T
+            forward[zh, place * 128 : place * 128 + 128] = both
     order = np.concatenate([np.arange(0, 448, 2), np.arange(1, 448, 2)])
     cos, sin = trig(np.arange(448), order, LATS)
     lat_forward = np.concatenate([cos, sin], axis=1)
-    lat_inverse = np.concatenate([cos.T, sin.T], axis=1)
-    place = np.zeros((2, 2, 256, 96))
-    for parity in range(2):
-        for j in range(192):
-            channel = (j + 64 * parity) % 192
-            place[parity, channel // 96, j, channel % 96] = 1.0
     cast = lambda a: jnp.asarray(a.astype(np.float32)).astype(BF)
-    return tuple(cast(a) for a in (forward, lat_forward, lat_inverse, inverse, place))
+    return cast(forward), cast(lat_forward)
 
 
 def gelu_pair(value):
@@ -87,10 +72,12 @@
 
 
 def body(
-    fields, cotangent, inner, outer, fwd, latf, latb, inv, place,
-    out, grad,
+    fields, cotangent, inner, outer, fwd, latf,
+    out, inner_grad, outer_grad,
     TS, PK, R, OWN, SND, ZR, SS, D, E, XB, ZB, HB, BB, UB, SL, AM, BM, W, SB, HR, GI, GO,
+    LB, IV, GL, GR, GS, GZ, GB, GA,
     tsem, raw_ss, rsem, z_ss, zsem, d_ss, dsem, w_ss, wsem, wz_ss, wzsem, o_ss, fsem, hsem, osem,
+    g1s, g1r, g2s, g2r, g3s, g3r, g4s, g4r,
 ):
     lat = lax.axis_index("lat")
     lon = lax.axis_index("lon")
@@ -172,11 +159,23 @@
         def _(jj, fc=fc):
             issue(fc, jj)
 
+    def spot_of(b, width):
+        rows = lax.broadcasted_iota(jnp.int32, (256, width), 0)
+        cols = lax.broadcasted_iota(jnp.int32, (256, width), 1)
+        hit = (lax.rem(rows + 64 * parity, 192) == 96 * b + cols) & (rows < 192) & (cols < 96)
+        return jnp.where(hit, 1.0, 0.0).astype(F32)
+
+    for part in range(2):
+        LB[:, 448 * part : 448 * part + 448] = (
+            latf[:, 448 * part : 448 * part + 448].astype(F32).T.astype(BF)
+        )
+    IV[...] = fwd[zh].astype(F32).T.astype(BF)
+
     for refs, target in ((inner, AM), (outer, BM)):
         for part in range(2):
             total = None
             for b in range(2):
-                spot = place[parity, b]
+                spot = spot_of(b, 96).astype(BF)
                 moved = dot_nt(dot(spot, refs[2 * y + b, part]).astype(BF), spot)
                 total = moved if total is None else total + moved
             total = total.astype(BF)
@@ -190,10 +189,13 @@
     def stage_b(t):
         fc = t // 7
         drain(R.at[t], rsem.at[t])
-        table = fwd[fc, zh]
+        table = fwd[zh]
+        ids = lax.broadcasted_iota(jnp.int32, (256, 384), 0)
+        first = (ids < 2) & (zh == 0) | (ids >= 128) & (ids < 130) & (zh == 1)
+        weight = jnp.where((fc == 0) | first, 1.0, 2.0)
         for i in range(2):
             data = jnp.concatenate([R[t, i, u].reshape(448, 128) for u in range(3)], axis=1)
-            part = dot(table, data)
+            part = dot(table, data) * weight
             OWN[t % 2, i] = part[0:128]
             SND[t, i] = part[128:256].astype(BF)
         send(SND.at[t], ZR.at[t], z_ss, zsem.at[t], zdev)
@@ -278,7 +280,7 @@
         XB[0:448, :] = z_adj.astype(BF)
         XB[448:896, 0:256] = (-z_adj[:, 256:512]).astype(BF)
         XB[448:896, 256:512] = z_adj[:, 0:256].astype(BF)
-        adj = dot(latb[...], XB[...])
+        adj = dot(LB[...], XB[...])
         for part in range(2):
             own = adj[:, 256 * part : 256 * part + 256]
             c0 = own[0:224, 128:256]
@@ -298,7 +300,7 @@
         for r in range(16):
             d2 = d_of(r)
             src = SB.at[d2, pl.ds(7 * half, 7)]
-            dst = W.at[pl.ds(7 * half, 7), zh * 16 + d]
+            dst = W.at[pl.ds(7 * half, 7), d]
             if r == 0:
                 pltpu.make_async_copy(src, dst, wsem.at[half]).start()
             else:
@@ -319,27 +321,37 @@
             else:
                 total = ref[0:256, 256:512] - ref[256:512, 0:256]
             for b in range(2):
-                spot = place[parity, b].astype(F32)
+                spot = spot_of(b, 128)
                 rows = lax.dot_general(
                     spot, total, (((0,), (0,)), ((), ())),
                     precision=lax.Precision.HIGHEST, preferred_element_type=F32,
                 )
-                grad[2 * kind + part, b] = lax.dot_general(
+                block = lax.dot_general(
                     rows, spot, (((1,), (0,)), ((), ())),
                     precision=lax.Precision.HIGHEST, preferred_element_type=F32,
                 )
+                at = 4 * (2 * kind + part) + 2 * b
+                GL[at] = block[0:48]
+                GL[at + 1] = block[48:96]
+
+    for r in range(16):
+        d2 = d_of(r)
+        if r == 0:
+            pltpu.make_async_copy(GL.at[d2], GR.at[d], g1r).start()
+        else:
+            send(GL.at[d2], GR.at[d], g1s, g1r, d_dev(d2))
 
     for half in range(2):
-        mine = W.at[pl.ds(7 * half, 7), pl.ds(16 * zh, 16)]
+        mine = W.at[pl.ds(7 * half, 7), pl.ds(0, 16)]
         drain(mine, wsem.at[half])
-        send(mine, mine, wz_ss, wzsem.at[half], zdev)
-
-    for half in range(2):
+        send(mine, W.at[pl.ds(7 * half, 7), pl.ds(16, 16)], wz_ss, wzsem.at[half], zdev)
+
+    def stage_e(half):
         drain(W.at[pl.ds(7 * half, 7), pl.ds(0, 16)], wzsem.at[half])
 
         @pl.loop(7 * half, 7 * half + 7)
         def _(g):
-            piece = dot(inv[zh], W[g].reshape(256, 384)).astype(BF)
+            piece = dot(IV[...], W[g].reshape(256, 384)).astype(BF)
             for u in range(3):
                 R[g, 0, u] = piece[:, 128 * u : 128 * u + 128].reshape(8, 56, 128)
             for r in range(8):
@@ -354,16 +366,48 @@
                     send(*full, o_ss, fsem, s_dev(s2))
                     send(*part, o_ss, hsem.at[g], s_dev(s2))
 
-    @pl.loop(0, 14)
-    def _(g):
-        drain(HR.at[:, :, g], hsem.at[g])
-        for kk in range(2):
-            for q in range(2):
-                first, second = swap_halves(
-                    HR[2 * q, kk, g].astype(F32), HR[2 * q + 1, kk, g].astype(F32)
-                )
-                TS[0, 14 * kk + g, 0, q] = first.astype(BF)
-                TS[0, 14 * kk + g, 1, q] = second.astype(BF)
+    def finish(low, high):
+        @pl.loop(low, high)
+        def _(g):
+            drain(HR.at[:, :, g], hsem.at[g])
+            for kk in range(2):
+                for q in range(2):
+                    first, second = swap_halves(
+                        HR[2 * q, kk, g].astype(F32), HR[2 * q + 1, kk, g].astype(F32)
+                    )
+                    TS[0, 14 * kk + g, 0, q] = first.astype(BF)
+                    TS[0, 14 * kk + g, 1, q] = second.astype(BF)
+
+    stage_e(0)
+    drain(GR, g1r)
+    GS[...] = jnp.sum(GR[...], axis=0)
+    send(GS, GZ, g2s, g2r, zdev)
+    stage_e(1)
+    drain(GZ, g2r)
+    GB[y] = ((GS[...] + GZ[...]) * (1.0 / math.sqrt(LATS * MODES))).astype(BF)
+    for r in range(1, 4):
+        send(GB.at[y], GB.at[y], g3s, g3r, s_dev((s + 2 * r) % 8))
+    finish(0, 4)
+    drain(GB.at[pl.ds(0, 3)], g3r)
+    for r in range(16):
+        d2 = d_of(r)
+        if r == 0:
+            pltpu.make_async_copy(GB, GA.at[d], g4r).start()
+        else:
+            send(GB, GA.at[d], g4s, g4r, d_dev(d2))
+    finish(4, 14)
+    drain(GA, g4r)
+    for kind, ref in enumerate((inner_grad, outer_grad)):
+        for part in range(2):
+            for b in range(2):
+                for h in range(2):
+                    at = 4 * (2 * kind + part) + 2 * b + h
+                    for y2 in range(4):
+                        ref[2 * y2 + b, part, 48 * h : 48 * h + 48, :] = GA[at, y2].astype(F32)[:, 0:96]
+    drain(GL.at[pl.ds(0, 15)], g1s)
+    drain(GS, g2s)
+    drain(GB.at[pl.ds(0, 3)], g3s)
+    drain(GA.at[pl.ds(0, 15)], g4s)
 
     for q in range(2):
         pltpu.make_async_copy(
@@ -406,17 +450,27 @@
         pltpu.VMEM((4, 2, 14, 56, 128), BF),
         pltpu.VMEM((512, 512), F32),
         pltpu.VMEM((512, 512), F32),
+        pltpu.VMEM((448, 896), BF),
+        pltpu.VMEM((448, 256), BF),
+        pltpu.VMEM((16, 48, 128), F32),
+        pltpu.VMEM((16, 48, 128), F32),
+        pltpu.VMEM((48, 128), F32),
+        pltpu.VMEM((48, 128), F32),
+        pltpu.VMEM((4, 48, 128), BF),
+        pltpu.VMEM((16, 4, 48, 128), BF),
         dma((2,)), dma, dma((14,)), dma, dma((14,)), dma, dma((2,)), dma, dma((2,)),
         dma, dma((2,)), dma, dma, dma((14,)), dma,
+        dma, dma, dma, dma, dma, dma, dma, dma,
     ]
     return pl.pallas_call(
         body,
         out_shape=(
             jax.ShapeDtypeStruct((28, 2, 56, 768), BF),
-            jax.ShapeDtypeStruct((4, 2, 96, 96), F32),
+            jax.ShapeDtypeStruct((BLOCKS, 2, BLOCK_W, BLOCK_W), F32),
+            jax.ShapeDtypeStruct((BLOCKS, 2, BLOCK_W, BLOCK_W), F32),
         ),
-        in_specs=[anyspace] * 2 + [vmem] * 7,
-        out_specs=(anyspace, vmem),
+        in_specs=[anyspace] * 2 + [vmem] * 4,
+        out_specs=(anyspace, vmem, vmem),
         scratch_shapes=scratch,
         compiler_params=pltpu.CompilerParams(
             collective_id=0, has_side_effects=True, vmem_limit_bytes=67043328
@@ -426,18 +480,13 @@
 
 
 def local(fields, cotangent, inner_weight, outer_weight):
-    field_gradient, part = step(
+    field_gradient, inner_gradient, outer_gradient = step(
         fields.reshape(28, 2, 56, 768),
         cotangent.reshape(28, 2, 56, 768),
         inner_weight,
         outer_weight,
     )
-    y = lax.axis_index("lon") % 8 // 2
-    part = part * (1.0 / math.sqrt(LATS * MODES))
-    part = part.reshape(2, 2, 2, BLOCK_W, BLOCK_W).transpose(0, 2, 1, 3, 4)
-    mine = jnp.where(jnp.arange(4)[None, :, None, None, None, None] == y, part[:, None], 0.0)
-    total = lax.psum(mine.reshape(2, BLOCKS, 2, BLOCK_W, BLOCK_W), ("lat", "lon"))
-    return field_gradient.reshape(fields.shape), total[0], total[1]
+    return field_gradient.reshape(fields.shape), inner_gradient, outer_gradient
 
 
 def solution(mesh):

time: 401 us -> 249 us (0.62)
  waiting for transfers between devices: 149 us -> 0 us
  Pallas kernels: 226 us -> 242 us
  between operations: 14.1 us -> 0.66 us
    psum x1 -> x0, waiting for transfers between devices: 149 us -> none  [local(): lax.psum(mine.reshape(2, BLOCKS, 2, BLOCK_W, BLOCK_W), ('lat', 'lon'))]
    pallas_call x1, Pallas kernels: 226 us -> 242 us  [step(): pl.pallas_call(body, out_shape=(jax.ShapeDtypeStruct((28, 2, 56, 768), BF...]
  transfers between devices with their start and end apart: 1 -> 0, of which waited for: 1 -> 0; matrix products, arithmetic and copies ran while one was open for 0% -> 0% of each run, Pallas kernels for 0% -> 0%
where the time goes in v2:
time: 249 us
  Pallas kernels  242 us (97%)
  local copies, waits for them, and re-layouts  6.78 us (3%)
    pallas_call x1, Pallas kernels, step(): pl.pallas_call(body, out_shape=(jax.ShapeDtypeStruct((28, 2, 56, 768), BF...  242 us
    unnamed x7, local copies, waits for them, and re-layouts  6.78 us

profile of v2, /device:TPU:1, one launch (start us, length us, event | category | flops | bytes accessed | tf_op | source)
XLA Modules:
  0.0 249.1 jit_solution(4056186196218770305)
XLA Ops:
  0.6 241.7 %spectral_step.1 = (bf16[28,2,56,768]{3,2,1,0:T(8,128)(2,1)}, f32[8,2,96,96]{3,2,1,0:T(8,128)}, f32[8,2,96,96]{3,2,1,0:T(8,128)}) custom-call(bf16[28,2,56,768]{3,2,1,0:T(8,128)(2,1)} %bitcast.3, bf16[28,2,56,768]{3,2,1,0:T(8,128)(2,1)} %bitcast.4, bf16[8,2,96,96]{3,2,1,0:T(8,128)(2,1)} %inner.1, bf16[8,2,96,96]{3,2,1,0:T(8,128)(2,1)} %outer.1, ...), custom_call_target="tpu_custom_call" | custom-call | tf_op jit(solution)/shard_map/spectral_step/pallas_call | solution.py:465
  242.3 0.0 copy-start.1
  242.4 0.0 copy-start
  242.4 5.0 %copy.12 = bf16[56,56,768]{2,1,0:T(8,128)(2,1)} copy(bf16[56,56,768]{2,1,0:T(8,128)(2,1)} %bitcast.5) | data formatting | bytes 9633792
  247.4 0.0 copy-done.1
  247.4 0.9 copy.13
  248.3 0.0 copy-done
  248.3 0.9 copy.14
Async XLA Ops:
  242.3 5.0 %copy-start.1 = (f32[8,2,96,96]{3,2,1,0:T(8,128)S(1)}, f32[8,2,96,96]{3,2,1,0:T(8,128)}, u32[]{:S(2)}) copy-start(f32[8,2,96,96]{3,2,1,0:T(8,128)} %get-tuple-element.13) | copy-start | bytes 1769476
  242.4 5.9 %copy-start = (f32[8,2,96,96]{3,2,1,0:T(8,128)S(1)}, f32[8,2,96,96]{3,2,1,0:T(8,128)}, u32[]{:S(2)}) copy-start(f32[8,2,96,96]{3,2,1,0:T(8,128)} %get-tuple-element.14) | copy-start | bytes 1769476

commit v3 on v2

--- a/solution.py
+++ b/solution.py
@@ -14,6 +14,10 @@
 BLOCKS = 8
 BLOCK_W = 96
 MESH = pl.DeviceIdType.MESH
+AHEAD = 2
+EARLY = 3
+GRAD_AT = (0, 4, 6, 8, 11)
+LAG = 1
 BF = jnp.bfloat16
 F32 = jnp.float32
 
@@ -72,12 +76,12 @@
 
 
 def body(
-    fields, cotangent, inner, outer, fwd, latf,
+    fields, cotangent, inner_any, outer_any, fwd_any, latf_any,
     out, inner_grad, outer_grad,
     TS, PK, R, OWN, SND, ZR, SS, D, E, XB, ZB, HB, BB, UB, SL, AM, BM, W, SB, HR, GI, GO,
-    LB, IV, GL, GR, GS, GZ, GB, GA,
+    LB, IV, GL, GR, GS, GZ, GB, GA, fwd, latf, inner, outer,
     tsem, raw_ss, rsem, z_ss, zsem, d_ss, dsem, w_ss, wsem, wz_ss, wzsem, o_ss, fsem, hsem, osem,
-    g1s, g1r, g2s, g2r, g3s, g3r, g4s, g4r,
+    g1s, g1r, g2s, g2r, g3s, g3r, g4s, g4r, psem,
 ):
     lat = lax.axis_index("lat")
     lon = lax.axis_index("lon")
@@ -118,6 +122,10 @@
                 sources[fc].at[:, :, :, pl.ds(128 + 384 * q, 128)], TS.at[fc, :, :, q], tsem.at[fc]
             ).start()
 
+    loads = ((fwd_any, fwd), (latf_any, latf), (inner_any, inner), (outer_any, outer))
+    for i, (src, dst) in enumerate(loads):
+        pltpu.make_async_copy(src, dst, psem.at[i]).start()
+
     barrier = pltpu.get_barrier_semaphore()
     for r in range(1, 8):
         pl.semaphore_signal(barrier, inc=1, device_id=s_dev(s_of(r)), device_id_type=MESH)
@@ -126,38 +134,47 @@
     pl.semaphore_signal(barrier, inc=1, device_id=zdev, device_id_type=MESH)
     pl.semaphore_wait(barrier, 23)
 
-    def issue(fc, jj):
+    def pack(fc, jj):
         for kk in range(2):
-            for i in range(2):
-                g = 14 * kk + 2 * jj + i
-                for q in range(2):
-                    even, odd = swap_halves(
-                        TS[fc, g, 0, q].astype(F32), TS[fc, g, 1, q].astype(F32)
-                    )
-                    PK[fc, g, 2 * q] = even.astype(BF)
-                    PK[fc, g, 2 * q + 1] = odd.astype(BF)
-        j = 7 * fc + jj
+            g = 14 * kk + jj
+            for q in range(2):
+                even, odd = swap_halves(TS[fc, g, 0, q].astype(F32), TS[fc, g, 1, q].astype(F32))
+                PK[fc, g, 2 * q] = even.astype(BF)
+                PK[fc, g, 2 * q + 1] = odd.astype(BF)
+
+    def send_raw(fc, jj, full):
+        j = 14 * fc + jj
         for r in range(8):
             s2 = s_of(r)
             y2 = s2 // 2
-            g0 = 14 * (s2 % 2) + 2 * jj
+            g0 = 14 * (s2 % 2) + jj
             lane = pl.multiple_of(128 * (3 * (y2 // 2) + 2 * (y2 % 2)), 128)
-            pairs = (
-                (sources[fc].at[pl.ds(g0, 2), :, :, pl.ds(lane, 128)], R.at[j, :, pl.ds(0, 2), s]),
-                (PK.at[fc, pl.ds(g0, 2), y2], R.at[j, :, 2, s]),
-            )
-            for src, dst in pairs:
-                if r == 0:
-                    pltpu.make_async_copy(src, dst, rsem.at[j]).start()
-                else:
-                    send(src, dst, raw_ss, rsem.at[j], s_dev(s2))
+            if full:
+                src, dst = sources[fc].at[g0, :, :, pl.ds(lane, 128)], R.at[j, pl.ds(0, 2), s]
+            else:
+                src, dst = PK.at[fc, g0, y2], R.at[j, 2, s]
+            if r == 0:
+                pltpu.make_async_copy(src, dst, rsem.at[j]).start()
+            else:
+                send(src, dst, raw_ss, rsem.at[j], s_dev(s2))
 
     for fc in range(2):
+        ahead = EARLY if fc == 0 else 0
+
+        @pl.loop(0, ahead)
+        def _(jj, fc=fc):
+            send_raw(fc, jj, True)
+
         drain(TS.at[fc], tsem.at[fc])
 
-        @pl.loop(0, 7)
-        def _(jj, fc=fc):
-            issue(fc, jj)
+        @pl.loop(0, 14)
+        def _(jj, fc=fc, ahead=ahead):
+            pack(fc, jj)
+            send_raw(fc, jj, False)
+
+            @pl.when(jj < 14 - ahead)
+            def _():
+                send_raw(fc, jj + ahead, True)
 
     def spot_of(b, width):
         rows = lax.broadcasted_iota(jnp.int32, (256, width), 0)
@@ -165,6 +182,8 @@
         hit = (lax.rem(rows + 64 * parity, 192) == 96 * b + cols) & (rows < 192) & (cols < 96)
         return jnp.where(hit, 1.0, 0.0).astype(F32)
 
+    for i, (src, dst) in enumerate(loads):
+        drain(dst, psem.at[i])
     for part in range(2):
         LB[:, 448 * part : 448 * part + 448] = (
             latf[:, 448 * part : 448 * part + 448].astype(F32).T.astype(BF)
@@ -187,30 +206,27 @@
                 target[256:512, 0:256] = -total
 
     def stage_b(t):
-        fc = t // 7
+        fc = t // 14
         drain(R.at[t], rsem.at[t])
-        table = fwd[zh]
         ids = lax.broadcasted_iota(jnp.int32, (256, 384), 0)
         first = (ids < 2) & (zh == 0) | (ids >= 128) & (ids < 130) & (zh == 1)
         weight = jnp.where((fc == 0) | first, 1.0, 2.0)
-        for i in range(2):
-            data = jnp.concatenate([R[t, i, u].reshape(448, 128) for u in range(3)], axis=1)
-            part = dot(table, data) * weight
-            OWN[t % 2, i] = part[0:128]
-            SND[t, i] = part[128:256].astype(BF)
+        data = jnp.concatenate([R[t, u].reshape(448, 128) for u in range(3)], axis=1)
+        part = dot(fwd[zh], data) * weight
+        SND[t] = part[128:256].astype(BF)
         send(SND.at[t], ZR.at[t], z_ss, zsem.at[t], zdev)
+        OWN[t % 2] = part[0:128]
 
     def stage_c(t):
-        fc = t // 7
-        jj = t % 7
+        fc = t // 14
+        jj = t % 14
         drain(ZR.at[t], zsem.at[t])
-        for i in range(2):
-            total = OWN[t % 2, i] + ZR[t, i].astype(F32)
-            SS[t, i] = total.astype(BF).reshape(16, 8, 384)
+        total = OWN[t % 2] + ZR[t].astype(F32)
+        SS[t] = total.astype(BF).reshape(16, 8, 384)
         for r in range(16):
             d2 = d_of(r)
-            src = SS.at[t, :, d2]
-            dst = D.at[fc, d, pl.ds(2 * jj, 2)]
+            src = SS.at[t, d2]
+            dst = D.at[fc, d, jj]
             if r == 0:
                 pltpu.make_async_copy(src, dst, dsem.at[fc]).start()
             else:
@@ -239,19 +255,15 @@
                 XB[0:448, 256:512] = whole.astype(BF)
                 XB[448:896, 0:256] = whole.astype(BF)
 
-    def fields_side():
-        unpack(0)
-
-        @pl.loop(0, 4)
-        def _(m):
-            spread(m)
-            z = dot(latf[...], XB[...]).astype(BF)
-            ZB[m] = z
-            gelu, slope = gelu_pair(dot(z, AM[...]))
-            HB[m] = gelu.astype(BF)
-            SL[m] = slope
-
-    @pl.loop(0, 10)
+    def fields_side(m):
+        spread(m)
+        z = dot(latf[...], XB[...]).astype(BF)
+        ZB[m] = z
+        gelu, slope = gelu_pair(dot(z, AM[...]))
+        HB[m] = gelu.astype(BF)
+        SL[m] = slope
+
+    @pl.loop(0, 18)
     def _(t):
         stage_b(t)
 
@@ -259,14 +271,23 @@
         def _():
             stage_c(t - 1)
 
-    fields_side()
-
-    @pl.loop(10, 14)
+    unpack(0)
+
+    @pl.loop(0, 4)
+    def _(m):
+        @pl.loop(18 + 2 * m, 20 + 2 * m)
+        def _(t):
+            stage_b(t)
+            stage_c(t - 1)
+
+        fields_side(m)
+
+    @pl.loop(26, 28)
     def _(t):
         stage_b(t)
         stage_c(t - 1)
 
-    stage_c(13)
+    stage_c(27)
     unpack(1)
 
     @pl.loop(0, 4)
@@ -290,81 +311,110 @@
             E[1, rows, :] = own[224:448, 0:128]
             E[2, rows, :] = jnp.where(low_half(c0.shape), c0, c1)
 
-    @pl.loop(0, 16)
-    def _(dd):
-        for u in range(3):
-            block = E[u, pl.ds(pl.multiple_of(112 * dd, 8), 112), :]
-            SB[dd, :, :, 128 * u : 128 * u + 128] = block.reshape(14, 8, 128).astype(BF)
-
-    for half in range(2):
+    def wsend(c):
+        for dd in range(16):
+            rows = pl.ds(pl.multiple_of(112 * dd + 8 * c, 8), 8)
+            for u in range(3):
+                SB[c, dd, :, 128 * u : 128 * u + 128] = E[u, rows, :].astype(BF)
         for r in range(16):
             d2 = d_of(r)
-            src = SB.at[d2, pl.ds(7 * half, 7)]
-            dst = W.at[pl.ds(7 * half, 7), d]
+            src = SB.at[c, d2]
+            dst = W.at[c, d]
             if r == 0:
-                pltpu.make_async_copy(src, dst, wsem.at[half]).start()
-            else:
-                send(src, dst, w_ss, wsem.at[half], d_dev(d2))
-
-    GI[...] = jnp.zeros_like(GI)
-    GO[...] = jnp.zeros_like(GO)
-
-    @pl.loop(0, 4)
-    def _(m):
-        GI[...] += dot_tn(ZB[m], UB[m])
-        GO[...] += dot_tn(HB[m], BB[m])
-
-    for kind, ref in enumerate((GI, GO)):
-        for part in range(2):
-            if part == 0:
-                total = ref[0:256, 0:256] + ref[256:512, 256:512]
-            else:
-                total = ref[0:256, 256:512] - ref[256:512, 0:256]
-            for b in range(2):
-                spot = spot_of(b, 128)
-                rows = lax.dot_general(
-                    spot, total, (((0,), (0,)), ((), ())),
-                    precision=lax.Precision.HIGHEST, preferred_element_type=F32,
-                )
-                block = lax.dot_general(
-                    rows, spot, (((1,), (0,)), ((), ())),
-                    precision=lax.Precision.HIGHEST, preferred_element_type=F32,
-                )
-                at = 4 * (2 * kind + part) + 2 * b
-                GL[at] = block[0:48]
-                GL[at + 1] = block[48:96]
-
-    for r in range(16):
-        d2 = d_of(r)
-        if r == 0:
-            pltpu.make_async_copy(GL.at[d2], GR.at[d], g1r).start()
-        else:
-            send(GL.at[d2], GR.at[d], g1s, g1r, d_dev(d2))
-
-    for half in range(2):
-        mine = W.at[pl.ds(7 * half, 7), pl.ds(0, 16)]
-        drain(mine, wsem.at[half])
-        send(mine, W.at[pl.ds(7 * half, 7), pl.ds(16, 16)], wz_ss, wzsem.at[half], zdev)
-
-    def stage_e(half):
-        drain(W.at[pl.ds(7 * half, 7), pl.ds(0, 16)], wzsem.at[half])
-
-        @pl.loop(7 * half, 7 * half + 7)
-        def _(g):
-            piece = dot(IV[...], W[g].reshape(256, 384)).astype(BF)
-            for u in range(3):
-                R[g, 0, u] = piece[:, 128 * u : 128 * u + 128].reshape(8, 56, 128)
-            for r in range(8):
-                s2 = s_of(r)
-                lane = pl.multiple_of(128 * my_tile, 128)
-                full = (R.at[g, 0, pl.ds(0, 2), s2], out.at[14 * core + g, :, :, pl.ds(lane, 128)])
-                part = (R.at[g, 0, 2, s2], HR.at[y, core, g])
-                if r == 0:
-                    pltpu.make_async_copy(*full, fsem).start()
-                    pltpu.make_async_copy(*part, hsem.at[g]).start()
+                pltpu.make_async_copy(src, dst, wsem.at[c]).start()
+            else:
+                send(src, dst, w_ss, wsem.at[c], d_dev(d2))
+
+    def relay(c):
+        mine = W.at[c, pl.ds(0, 16)]
+        drain(mine, wsem.at[c])
+        send(mine, W.at[c, pl.ds(16, 16)], wz_ss, wzsem.at[c], zdev)
+
+    def stage_e(g):
+        drain(W.at[g, pl.ds(16, 16)], wzsem.at[g])
+        piece = dot(IV[...], W[g].reshape(256, 384)).astype(BF)
+        for u in range(3):
+            R[g, u] = piece[:, 128 * u : 128 * u + 128].reshape(8, 56, 128)
+        for r in range(8):
+            s2 = s_of(r)
+            lane = pl.multiple_of(128 * my_tile, 128)
+            full = (R.at[g, pl.ds(0, 2), s2], out.at[14 * core + g, :, :, pl.ds(lane, 128)])
+            part = (R.at[g, 2, s2], HR.at[y, core, g])
+            if r == 0:
+                pltpu.make_async_copy(*full, fsem).start()
+                pltpu.make_async_copy(*part, hsem.at[g]).start()
+            else:
+                send(*full, o_ss, fsem, s_dev(s2))
+                send(*part, o_ss, hsem.at[g], s_dev(s2))
+
+    def weight_piece(kind, i, j):
+        left = (ZB, HB)[kind][:, :, 256 * i : 256 * i + 256].reshape(1792, 256)
+        right = (UB, BB)[kind][:, :, 256 * j : 256 * j + 256].reshape(1792, 256)
+        (GI, GO)[kind][256 * i : 256 * i + 256, 256 * j : 256 * j + 256] = dot_tn(left, right)
+
+    def collect():
+        for kind, ref in enumerate((GI, GO)):
+            for part in range(2):
+                if part == 0:
+                    total = ref[0:256, 0:256] + ref[256:512, 256:512]
                 else:
-                    send(*full, o_ss, fsem, s_dev(s2))
-                    send(*part, o_ss, hsem.at[g], s_dev(s2))
+                    total = ref[0:256, 256:512] - ref[256:512, 0:256]
+                for b in range(2):
+                    spot = spot_of(b, 128).astype(BF)
+                    rows = dot_tn(spot, total.astype(BF)).astype(BF)
+                    block = dot(rows, spot)
+                    at = 4 * (2 * kind + part) + 2 * b
+                    GL[at] = block[0:48]
+                    GL[at + 1] = block[48:96]
+        for r in range(16):
+            d2 = d_of(r)
+            if r == 0:
+                pltpu.make_async_copy(GL.at[d2], GR.at[d], g1r).start()
+            else:
+                send(GL.at[d2], GR.at[d], g1s, g1r, d_dev(d2))
+
+    def sum_rows():
+        drain(GR, g1r)
+        GS[...] = jnp.sum(GR[...], axis=0)
+        send(GS, GZ, g2s, g2r, zdev)
+
+    def sum_half():
+        drain(GZ, g2r)
+        GB[y] = ((GS[...] + GZ[...]) * (1.0 / math.sqrt(LATS * MODES))).astype(BF)
+        for r in range(1, 4):
+            send(GB.at[y], GB.at[y], g3s, g3r, s_dev((s + 2 * r) % 8))
+
+    def spread_out():
+        drain(GB.at[pl.ds(0, 3)], g3r)
+        for r in range(16):
+            d2 = d_of(r)
+            if r == 0:
+                pltpu.make_async_copy(GB, GA.at[d], g4r).start()
+            else:
+                send(GB, GA.at[d], g4s, g4r, d_dev(d2))
+
+    for c in range(AHEAD):
+        wsend(c)
+
+    @pl.loop(0, 14)
+    def _(c):
+        @pl.when(c < 14 - AHEAD)
+        def _():
+            wsend(c + AHEAD)
+
+        relay(c)
+
+        @pl.when(c >= LAG)
+        def _():
+            stage_e(c - LAG)
+
+        for i in range(8):
+            @pl.when(c == GRAD_AT[0] + i // 2)
+            def _(i=i):
+                weight_piece(i // 4, i // 2 % 2, i % 2)
+
+        for at, action in zip(GRAD_AT[1:], (collect, sum_rows, sum_half, spread_out)):
+            pl.when(c == at)(action)
 
     def finish(low, high):
         @pl.loop(low, high)
@@ -378,24 +428,11 @@
                     TS[0, 14 * kk + g, 0, q] = first.astype(BF)
                     TS[0, 14 * kk + g, 1, q] = second.astype(BF)
 
-    stage_e(0)
-    drain(GR, g1r)
-    GS[...] = jnp.sum(GR[...], axis=0)
-    send(GS, GZ, g2s, g2r, zdev)
-    stage_e(1)
-    drain(GZ, g2r)
-    GB[y] = ((GS[...] + GZ[...]) * (1.0 / math.sqrt(LATS * MODES))).astype(BF)
-    for r in range(1, 4):
-        send(GB.at[y], GB.at[y], g3s, g3r, s_dev((s + 2 * r) % 8))
-    finish(0, 4)
-    drain(GB.at[pl.ds(0, 3)], g3r)
-    for r in range(16):
-        d2 = d_of(r)
-        if r == 0:
-            pltpu.make_async_copy(GB, GA.at[d], g4r).start()
-        else:
-            send(GB, GA.at[d], g4s, g4r, d_dev(d2))
-    finish(4, 14)
+    @pl.loop(14 - LAG, 14)
+    def _(g):
+        stage_e(g)
+
+    finish(0, 14)
     drain(GA, g4r)
     for kind, ref in enumerate((inner_grad, outer_grad)):
         for part in range(2):
@@ -415,12 +452,12 @@
         ).start()
     drain(TS.at[0], osem)
     drain(out.at[:, :, :, pl.ds(0, 512)], fsem)
-    drain(R.at[:, :, :, pl.ds(0, 7)], raw_ss)
+    drain(R.at[:, :, pl.ds(0, 7)], raw_ss)
     drain(SND, z_ss)
-    drain(SS.at[:, :, pl.ds(0, 15)], d_ss)
-    drain(SB.at[pl.ds(0, 15)], w_ss)
+    drain(SS.at[:, pl.ds(0, 15)], d_ss)
+    drain(SB.at[:, pl.ds(0, 15)], w_ss)
     drain(W.at[:, pl.ds(0, 16)], wz_ss)
-    drain(R.at[:, 0, :, pl.ds(0, 7)], o_ss)
+    drain(R.at[pl.ds(0, 14), :, pl.ds(0, 7)], o_ss)
 
 
 def step(fields, cotangent, inner, outer):
@@ -430,11 +467,11 @@
     scratch = [
         pltpu.VMEM((2, 28, 2, 2, 56, 128), BF),
         pltpu.VMEM((2, 28, 4, 56, 128), BF),
-        pltpu.VMEM((14, 2, 3, 8, 56, 128), BF),
-        pltpu.VMEM((2, 2, 128, 384), F32),
-        pltpu.VMEM((14, 2, 128, 384), BF),
-        pltpu.VMEM((14, 2, 128, 384), BF),
-        pltpu.VMEM((14, 2, 16, 8, 384), BF),
+        pltpu.VMEM((28, 3, 8, 56, 128), BF),
+        pltpu.VMEM((2, 128, 384), F32),
+        pltpu.VMEM((28, 128, 384), BF),
+        pltpu.VMEM((28, 128, 384), BF),
+        pltpu.VMEM((28, 16, 8, 384), BF),
         pltpu.VMEM((2, 16, 14, 8, 384), BF),
         pltpu.VMEM((3, 1792, 128), F32),
         pltpu.VMEM((896, 512), BF),
@@ -446,7 +483,7 @@
         pltpu.VMEM((512, 512), BF),
         pltpu.VMEM((512, 512), BF),
         pltpu.VMEM((14, 32, 8, 384), BF),
-        pltpu.VMEM((16, 14, 8, 384), BF),
+        pltpu.VMEM((14, 16, 8, 384), BF),
         pltpu.VMEM((4, 2, 14, 56, 128), BF),
         pltpu.VMEM((512, 512), F32),
         pltpu.VMEM((512, 512), F32),
@@ -458,9 +495,13 @@
         pltpu.VMEM((48, 128), F32),
         pltpu.VMEM((4, 48, 128), BF),
         pltpu.VMEM((16, 4, 48, 128), BF),
-        dma((2,)), dma, dma((14,)), dma, dma((14,)), dma, dma((2,)), dma, dma((2,)),
-        dma, dma((2,)), dma, dma, dma((14,)), dma,
-        dma, dma, dma, dma, dma, dma, dma, dma,
+        pltpu.VMEM((2, 256, 448), BF),
+        pltpu.VMEM((448, 896), BF),
+        pltpu.VMEM((BLOCKS, 2, BLOCK_W, BLOCK_W), BF),
+        pltpu.VMEM((BLOCKS, 2, BLOCK_W, BLOCK_W), BF),
+        dma((2,)), dma, dma((28,)), dma, dma((28,)), dma, dma((2,)), dma, dma((14,)),
+        dma, dma((14,)), dma, dma, dma((14,)), dma,
+        dma, dma, dma, dma, dma, dma, dma, dma, dma((4,)),
     ]
     return pl.pallas_call(
         body,
@@ -469,7 +510,7 @@
             jax.ShapeDtypeStruct((BLOCKS, 2, BLOCK_W, BLOCK_W), F32),
             jax.ShapeDtypeStruct((BLOCKS, 2, BLOCK_W, BLOCK_W), F32),
         ),
-        in_specs=[anyspace] * 2 + [vmem] * 4,
+        in_specs=[anyspace] * 6,
         out_specs=(anyspace, vmem, vmem),
         scratch_shapes=scratch,
         compiler_params=pltpu.CompilerParams(

time: 249 us -> 216 us (0.87)
  Pallas kernels: 242 us -> 208 us
    pallas_call x1, Pallas kernels: 242 us -> 208 us  [step(): pl.pallas_call(body, out_shape=(jax.ShapeDtypeStruct((28, 2, 56, 768), BF...]
where the time goes in v3:
time: 216 us
  Pallas kernels  208 us (96%)
  local copies, waits for them, and re-layouts  6.78 us (3%)
    pallas_call x1, Pallas kernels, step(): pl.pallas_call(body, out_shape=(jax.ShapeDtypeStruct((28, 2, 56, 768), BF...  208 us
    unnamed x7, local copies, waits for them, and re-layouts  6.78 us

profile of v3, /device:TPU:1, one launch (start us, length us, event | category | flops | bytes accessed | tf_op | source)
XLA Modules:
  0.0 215.7 jit_solution(10497717224097137580)
XLA Ops:
  0.6 208.3 %spectral_step.1 = (bf16[28,2,56,768]{3,2,1,0:T(8,128)(2,1)}, f32[8,2,96,96]{3,2,1,0:T(8,128)}, f32[8,2,96,96]{3,2,1,0:T(8,128)}) custom-call(bf16[28,2,56,768]{3,2,1,0:T(8,128)(2,1)} %bitcast.3, bf16[28,2,56,768]{3,2,1,0:T(8,128)(2,1)} %bitcast.4, bf16[8,2,96,96]{3,2,1,0:T(8,128)(2,1)} %inner_any.1, bf16[8,2,96,96]{3,2,1,0:T(8,128)(2,1)} %outer_any.1, ...), custom_call_target="tpu_custom_call" | custom-call | tf_op jit(solution)/shard_map/spectral_step/pallas_call | solution.py:506
  208.9 0.0 copy-start.1
  208.9 0.0 copy-start
  208.9 5.0 %copy.12 = bf16[56,56,768]{2,1,0:T(8,128)(2,1)} copy(bf16[56,56,768]{2,1,0:T(8,128)(2,1)} %bitcast.5) | data formatting | bytes 9633792
  213.9 0.0 copy-done.1
  214.0 0.9 copy.13
  214.8 0.0 copy-done
  214.8 0.9 copy.14
Async XLA Ops:
  208.9 5.0 %copy-start.1 = (f32[8,2,96,96]{3,2,1,0:T(8,128)S(1)}, f32[8,2,96,96]{3,2,1,0:T(8,128)}, u32[]{:S(2)}) copy-start(f32[8,2,96,96]{3,2,1,0:T(8,128)} %get-tuple-element.13) | copy-start | bytes 1769476
  208.9 5.9 %copy-start = (f32[8,2,96,96]{3,2,1,0:T(8,128)S(1)}, f32[8,2,96,96]{3,2,1,0:T(8,128)}, u32[]{:S(2)}) copy-start(f32[8,2,96,96]{3,2,1,0:T(8,128)} %get-tuple-element.14) | copy-start | bytes 1769476

commit v4 on v3

--- a/solution.py
+++ b/solution.py
@@ -15,9 +15,9 @@
 BLOCK_W = 96
 MESH = pl.DeviceIdType.MESH
 AHEAD = 2
-EARLY = 3
-GRAD_AT = (0, 4, 6, 8, 11)
-LAG = 1
+EARLY = 1
+GRAD_AT = (0, 4, 6, 8, 10, 12)
+LAG = 2
 BF = jnp.bfloat16
 F32 = jnp.float32
 
@@ -79,9 +79,9 @@
     fields, cotangent, inner_any, outer_any, fwd_any, latf_any,
     out, inner_grad, outer_grad,
     TS, PK, R, OWN, SND, ZR, SS, D, E, XB, ZB, HB, BB, UB, SL, AM, BM, W, SB, HR, GI, GO,
-    LB, IV, GL, GR, GS, GZ, GB, GA, fwd, latf, inner, outer,
+    LB, IV, GL, GR, GS, GT, GY, GZ, GB, GA, fwd, latf, inner, outer,
     tsem, raw_ss, rsem, z_ss, zsem, d_ss, dsem, w_ss, wsem, wz_ss, wzsem, o_ss, fsem, hsem, osem,
-    g1s, g1r, g2s, g2r, g3s, g3r, g4s, g4r, psem,
+    g1s, g1r, g2s, g2r, g5s, g5r, g3s, g3r, g4s, g4r, psem,
 ):
     lat = lax.axis_index("lat")
     lon = lax.axis_index("lon")
@@ -93,12 +93,22 @@
     d = 2 * lat + core
     my_tile = 3 * (y // 2) + 2 * parity
     zdev = (lat, (1 - zh) * 8 + s)
+    x = lat % 4
+    zl = lat // 4
+    own = 2 * x + core
+    ldev = ((1 - zl) * 4 + x, lon)
 
     def s_of(r):
         return (s + r) % 8
 
     def d_of(r):
         return (d + r) % 16
+
+    def o_of(r):
+        return (own + r) % 8
+
+    def o_dev(o2):
+        return (zl * 4 + o2 // 2, zh * 8 + y * 2 + o2 % 2)
 
     def s_dev(s2):
         return (lat, zh * 8 + s2)
@@ -363,35 +373,38 @@
                     spot = spot_of(b, 128).astype(BF)
                     rows = dot_tn(spot, total.astype(BF)).astype(BF)
                     block = dot(rows, spot)
-                    at = 4 * (2 * kind + part) + 2 * b
-                    GL[at] = block[0:48]
-                    GL[at + 1] = block[48:96]
-        for r in range(16):
-            d2 = d_of(r)
+                    GL[2 * (2 * kind + part) + b] = block[0:96].astype(BF)
+        for r in range(8):
+            o2 = o_of(r)
             if r == 0:
-                pltpu.make_async_copy(GL.at[d2], GR.at[d], g1r).start()
-            else:
-                send(GL.at[d2], GR.at[d], g1s, g1r, d_dev(d2))
+                pltpu.make_async_copy(GL.at[o2], GR.at[own], g1r).start()
+            else:
+                send(GL.at[o2], GR.at[own], g1s, g1r, o_dev(o2))
 
     def sum_rows():
         drain(GR, g1r)
-        GS[...] = jnp.sum(GR[...], axis=0)
-        send(GS, GZ, g2s, g2r, zdev)
-
-    def sum_half():
-        drain(GZ, g2r)
-        GB[y] = ((GS[...] + GZ[...]) * (1.0 / math.sqrt(LATS * MODES))).astype(BF)
+        GS[...] = jnp.sum(GR[...].astype(F32), axis=0)
+        send(GS, GY, g2s, g2r, ldev)
+
+    def sum_near():
+        drain(GY, g2r)
+        GT[...] = GS[...] + GY[...]
+        send(GT, GZ, g5s, g5r, zdev)
+
+    def sum_far():
+        drain(GZ, g5r)
+        GB[y] = ((GT[...] + GZ[...]) * (1.0 / math.sqrt(LATS * MODES))).astype(BF)
         for r in range(1, 4):
             send(GB.at[y], GB.at[y], g3s, g3r, s_dev((s + 2 * r) % 8))
 
     def spread_out():
         drain(GB.at[pl.ds(0, 3)], g3r)
-        for r in range(16):
-            d2 = d_of(r)
+        for r in range(8):
+            o2 = o_of(r)
             if r == 0:
-                pltpu.make_async_copy(GB, GA.at[d], g4r).start()
-            else:
-                send(GB, GA.at[d], g4s, g4r, d_dev(d2))
+                pltpu.make_async_copy(GB, GA.at[own], g4r).start()
+            else:
+                send(GB, GA.at[own], g4s, g4r, o_dev(o2))
 
     for c in range(AHEAD):
         wsend(c)
@@ -413,7 +426,7 @@
             def _(i=i):
                 weight_piece(i // 4, i // 2 % 2, i % 2)
 
-        for at, action in zip(GRAD_AT[1:], (collect, sum_rows, sum_half, spread_out)):
+        for at, action in zip(GRAD_AT[1:], (collect, sum_rows, sum_near, sum_far, spread_out)):
             pl.when(c == at)(action)
 
     def finish(low, high):
@@ -427,6 +440,10 @@
                     )
                     TS[0, 14 * kk + g, 0, q] = first.astype(BF)
                     TS[0, 14 * kk + g, 1, q] = second.astype(BF)
+                    pltpu.make_async_copy(
+                        TS.at[0, 14 * kk + g, :, q],
+                        out.at[14 * kk + g, :, :, pl.ds(128 + 384 * q, 128)], osem,
+                    ).start()
 
     @pl.loop(14 - LAG, 14)
     def _(g):
@@ -437,19 +454,15 @@
     for kind, ref in enumerate((inner_grad, outer_grad)):
         for part in range(2):
             for b in range(2):
-                for h in range(2):
-                    at = 4 * (2 * kind + part) + 2 * b + h
-                    for y2 in range(4):
-                        ref[2 * y2 + b, part, 48 * h : 48 * h + 48, :] = GA[at, y2].astype(F32)[:, 0:96]
-    drain(GL.at[pl.ds(0, 15)], g1s)
+                at = 2 * (2 * kind + part) + b
+                for y2 in range(4):
+                    ref[2 * y2 + b, part] = GA[at, y2].astype(F32)[:, 0:96]
+    drain(GL.at[pl.ds(0, 7)], g1s)
     drain(GS, g2s)
+    drain(GT, g5s)
     drain(GB.at[pl.ds(0, 3)], g3s)
-    drain(GA.at[pl.ds(0, 15)], g4s)
-
-    for q in range(2):
-        pltpu.make_async_copy(
-            TS.at[0, :, :, q], out.at[:, :, :, pl.ds(128 + 384 * q, 128)], osem
-        ).start()
+    drain(GA.at[pl.ds(0, 7)], g4s)
+
     drain(TS.at[0], osem)
     drain(out.at[:, :, :, pl.ds(0, 512)], fsem)
     drain(R.at[:, :, pl.ds(0, 7)], raw_ss)
@@ -489,19 +502,21 @@
         pltpu.VMEM((512, 512), F32),
         pltpu.VMEM((448, 896), BF),
         pltpu.VMEM((448, 256), BF),
-        pltpu.VMEM((16, 48, 128), F32),
-        pltpu.VMEM((16, 48, 128), F32),
-        pltpu.VMEM((48, 128), F32),
-        pltpu.VMEM((48, 128), F32),
-        pltpu.VMEM((4, 48, 128), BF),
-        pltpu.VMEM((16, 4, 48, 128), BF),
+        pltpu.VMEM((8, 96, 128), BF),
+        pltpu.VMEM((8, 96, 128), BF),
+        pltpu.VMEM((96, 128), F32),
+        pltpu.VMEM((96, 128), F32),
+        pltpu.VMEM((96, 128), F32),
+        pltpu.VMEM((96, 128), F32),
+        pltpu.VMEM((4, 96, 128), BF),
+        pltpu.VMEM((8, 4, 96, 128), BF),
         pltpu.VMEM((2, 256, 448), BF),
         pltpu.VMEM((448, 896), BF),
         pltpu.VMEM((BLOCKS, 2, BLOCK_W, BLOCK_W), BF),
         pltpu.VMEM((BLOCKS, 2, BLOCK_W, BLOCK_W), BF),
         dma((2,)), dma, dma((28,)), dma, dma((28,)), dma, dma((2,)), dma, dma((14,)),
         dma, dma((14,)), dma, dma, dma((14,)), dma,
-        dma, dma, dma, dma, dma, dma, dma, dma, dma((4,)),
+        dma, dma, dma, dma, dma, dma, dma, dma, dma, dma, dma((4,)),
     ]
     return pl.pallas_call(
         body,

time: 216 us -> 208 us (0.963)
  Pallas kernels: 208 us -> 200 us
    pallas_call x1, Pallas kernels: 208 us -> 200 us  [step(): pl.pallas_call(body, out_shape=(jax.ShapeDtypeStruct((28, 2, 56, 768), BF...]
where the time goes in v4:
time: 208 us; the launch traced here: 207 us
  Pallas kernels  200 us (96%)
  local copies, waits for them, and re-layouts  6.78 us (3%)
    pallas_call x1, Pallas kernels, step(): pl.pallas_call(body, out_shape=(jax.ShapeDtypeStruct((28, 2, 56, 768), BF...  200 us
    unnamed x7, local copies, waits for them, and re-layouts  6.78 us

profile of v4, /device:TPU:1, one launch (start us, length us, event | category | flops | bytes accessed | tf_op | source)
XLA Modules:
  0.0 207.5 jit_solution(2172515746286551004)
XLA Ops:
  0.6 200.0 %spectral_step.1 = (bf16[28,2,56,768]{3,2,1,0:T(8,128)(2,1)}, f32[8,2,96,96]{3,2,1,0:T(8,128)}, f32[8,2,96,96]{3,2,1,0:T(8,128)}) custom-call(bf16[28,2,56,768]{3,2,1,0:T(8,128)(2,1)} %bitcast.3, bf16[28,2,56,768]{3,2,1,0:T(8,128)(2,1)} %bitcast.4, bf16[8,2,96,96]{3,2,1,0:T(8,128)(2,1)} %inner_any.1, bf16[8,2,96,96]{3,2,1,0:T(8,128)(2,1)} %outer_any.1, ...), custom_call_target="tpu_custom_call" | custom-call | tf_op jit(solution)/shard_map/spectral_step/pallas_call | solution.py:521
  200.7 0.0 copy-start.1
  200.7 0.0 copy-start
  200.7 5.0 %copy.12 = bf16[56,56,768]{2,1,0:T(8,128)(2,1)} copy(bf16[56,56,768]{2,1,0:T(8,128)(2,1)} %bitcast.5) | data formatting | bytes 9633792
  205.7 0.0 copy-done.1
  205.7 0.9 copy.13
  206.6 0.0 copy-done
  206.6 0.9 copy.14
Async XLA Ops:
  200.7 5.0 %copy-start.1 = (f32[8,2,96,96]{3,2,1,0:T(8,128)S(1)}, f32[8,2,96,96]{3,2,1,0:T(8,128)}, u32[]{:S(2)}) copy-start(f32[8,2,96,96]{3,2,1,0:T(8,128)} %get-tuple-element.13) | copy-start | bytes 1769476
  200.7 5.9 %copy-start = (f32[8,2,96,96]{3,2,1,0:T(8,128)S(1)}, f32[8,2,96,96]{3,2,1,0:T(8,128)}, u32[]{:S(2)}) copy-start(f32[8,2,96,96]{3,2,1,0:T(8,128)} %get-tuple-element.14) | copy-start | bytes 1769476

commit v5 on v4

--- a/solution.py
+++ b/solution.py
@@ -273,7 +273,7 @@
         HB[m] = gelu.astype(BF)
         SL[m] = slope
 
-    @pl.loop(0, 18)
+    @pl.loop(0, 16)
     def _(t):
         stage_b(t)
 
@@ -285,14 +285,14 @@
 
     @pl.loop(0, 4)
     def _(m):
-        @pl.loop(18 + 2 * m, 20 + 2 * m)
+        @pl.loop(16 + 2 * m, 18 + 2 * m)
         def _(t):
             stage_b(t)
             stage_c(t - 1)
 
         fields_side(m)
 
-    @pl.loop(26, 28)
+    @pl.loop(24, 28)
     def _(t):
         stage_b(t)
         stage_c(t - 1)

time: 208 us -> 208 us (level)
  no operation moved by 1% of the time
where the time goes in v5:
time: 208 us
  Pallas kernels  200 us (96%)
  local copies, waits for them, and re-layouts  6.78 us (3%)
    pallas_call x1, Pallas kernels, step(): pl.pallas_call(body, out_shape=(jax.ShapeDtypeStruct((28, 2, 56, 768), BF...  200 us
    unnamed x7, local copies, waits for them, and re-layouts  6.78 us

profile of v5, /device:TPU:1, one launch (start us, length us, event | category | flops | bytes accessed | tf_op | source)
XLA Modules:
  0.0 207.7 jit_solution(10789856005794558880)
XLA Ops:
  0.6 200.3 %spectral_step.1 = (bf16[28,2,56,768]{3,2,1,0:T(8,128)(2,1)}, f32[8,2,96,96]{3,2,1,0:T(8,128)}, f32[8,2,96,96]{3,2,1,0:T(8,128)}) custom-call(bf16[28,2,56,768]{3,2,1,0:T(8,128)(2,1)} %bitcast.3, bf16[28,2,56,768]{3,2,1,0:T(8,128)(2,1)} %bitcast.4, bf16[8,2,96,96]{3,2,1,0:T(8,128)(2,1)} %inner_any.1, bf16[8,2,96,96]{3,2,1,0:T(8,128)(2,1)} %outer_any.1, ...), custom_call_target="tpu_custom_call" | custom-call | tf_op jit(solution)/shard_map/spectral_step/pallas_call | solution.py:521
  201.0 0.0 copy-start.1
  201.0 0.0 copy-start
  201.0 5.0 %copy.12 = bf16[56,56,768]{2,1,0:T(8,128)(2,1)} copy(bf16[56,56,768]{2,1,0:T(8,128)(2,1)} %bitcast.5) | data formatting | bytes 9633792
  206.0 0.0 copy-done.1
  206.0 0.9 copy.13
  206.9 0.0 copy-done
  206.9 0.9 copy.14
Async XLA Ops:
  201.0 5.0 %copy-start.1 = (f32[8,2,96,96]{3,2,1,0:T(8,128)S(1)}, f32[8,2,96,96]{3,2,1,0:T(8,128)}, u32[]{:S(2)}) copy-start(f32[8,2,96,96]{3,2,1,0:T(8,128)} %get-tuple-element.13) | copy-start | bytes 1769476
  201.0 5.9 %copy-start = (f32[8,2,96,96]{3,2,1,0:T(8,128)S(1)}, f32[8,2,96,96]{3,2,1,0:T(8,128)}, u32[]{:S(2)}) copy-start(f32[8,2,96,96]{3,2,1,0:T(8,128)} %get-tuple-element.14) | copy-start | bytes 1769476
